TPU v7x, 256 devices: a whole 4x4x8 slice. The times are simulated.
256 devices in a mesh: src: 4 (over y), snk: 8 (over z_hi, x), slab: 8 (over z_lo, core).
Axes of the slice: x: 4, y: 4, z: 8 (z_hi: 2, z_lo: 4; z = z_hi * 4 + z_lo), core: 2. Of those that a mesh axis runs over, the one named last changes fastest.
Arguments:
- eigvecs: bfloat16 [16, 32768, 384], P('snk', ('src', 'slab')), may hold values from -0.09375 to 0.09375
- perambulator: bfloat16 [16, 8, 4, 192, 384], P('snk', 'src'), may hold values from -0.4375 to 0.4375
- momenta: int32 [4, 3], replicated, may hold values from 1 to 3
- source_times: int32 [8], P('src'), may hold values from 0 to 15, as said below
Outputs:
- blocks: float32 [4, 16, 8, 4, 192, 384], P(None, 'snk', 'src', None, 'slab')
Inputs may be any that keep to these rules, and one draw needn't show every extreme that they name: `source_times`: distinct time slices.
All inputs are finite; a program needn't handle non-finite values.
Results may differ from a plain program's by a relative error of at most 0.0062.
Values may be sent and summed in bfloat16 or wider, within the bound.
A program may use at most 64 MiB of HBM per device.

v0:
```python
import math

import jax
import jax.numpy as jnp
from jax import lax
from jax.sharding import PartitionSpec as P

LX = 32
LY = 32
ZPL = 1


def split_up(shard, dim, length):
    lengths = shard.shape
    parts = shard.reshape(*lengths[:dim], length, lengths[dim] // length, *lengths[dim + 1 :])
    return jnp.moveaxis(parts, dim, 0)


def summed_on_arrival(shard, axis, dim):
    parts = split_up(shard, dim, lax.axis_size(axis))
    arrived = lax.all_to_all(parts, axis, split_axis=0, concat_axis=0, tiled=True)
    return arrived.sum(axis=0)


def laid_out(parts, dim):
    lengths = list(parts.shape[1:])
    lengths[dim] *= parts.shape[0]
    return jnp.moveaxis(parts, 0, dim).reshape(lengths)


def copy_for_each(shard, axis):
    copies = jnp.broadcast_to(shard, (lax.axis_size(axis), *shard.shape))
    return lax.all_to_all(copies, axis, split_axis=0, concat_axis=0, tiled=True)


def gather_directly(shard, axis, dim):
    return laid_out(copy_for_each(shard, axis), dim)


def over_copies(shard, axis):
    return copy_for_each(shard, axis).astype(jnp.float32).sum(axis=0)


def angles(momenta, xs, ys, zs, lz):
    fx = (momenta[:, 0:1] * xs[None, :] % LX).astype(jnp.float32) / LX
    fy = (momenta[:, 1:2] * ys[None, :] % LY).astype(jnp.float32) / LY
    fz = (momenta[:, 2:3] * zs[None, :] % lz).astype(jnp.float32) / lz
    return 2.0 * math.pi * (fx + fy + fz)


def local(eigvecs, perambulator, momenta, source_times):
    nev = eigvecs.shape[2] // 2
    count = eigvecs.shape[1]
    slabs = lax.axis_size("slab")
    lz = ZPL * lax.axis_size("src") * slabs
    sites = jnp.arange(count, dtype=jnp.int32)
    xs = sites % LX
    ys = sites // LX % LY
    zs = sites // (LX * LY) + lax.axis_index(("src", "slab")) * ZPL
    angle = angles(momenta, xs, ys, zs, lz)
    vreal = eigvecs[:, :, :nev].astype(jnp.float32)
    vimag = eigvecs[:, :, nev:].astype(jnp.float32)
    partials = []
    for m in range(angle.shape[0]):
        cosine = jnp.cos(angle[m])[None, :, None]
        sine = jnp.sin(angle[m])[None, :, None]
        phased = jnp.concatenate(
            [cosine * vreal + sine * vimag, cosine * vimag - sine * vreal], axis=2
        ).astype(jnp.bfloat16)
        gram = jnp.einsum("tsa,tsb->tab", eigvecs, phased, preferred_element_type=jnp.float32)
        real = gram[:, :nev, :nev] + gram[:, nev:, nev:]
        imag = gram[:, :nev, nev:] - gram[:, nev:, :nev]
        partials.append(jnp.concatenate([real, imag], axis=2))
    partial_value = jnp.stack(partials, axis=1)
    tdev = partial_value.shape[0]
    rows = nev // slabs
    local_times = lax.axis_index("snk") * tdev + jnp.arange(tdev, dtype=jnp.int32)
    slab_part = lax.psum_scatter(partial_value, "slab", scatter_dimension=2, tiled=True)
    share = summed_on_arrival(slab_part, "src", 2).astype(jnp.bfloat16)
    sink = gather_directly(share, "src", 2)
    selector = (source_times[:, None] == local_times[None, :]).astype(jnp.bfloat16)
    term = jnp.dot(selector, sink.reshape(tdev, -1), preferred_element_type=jnp.float32)
    picked = over_copies(term.astype(jnp.bfloat16), "snk").astype(jnp.float32).astype(jnp.bfloat16)
    picked = picked.reshape((source_times.shape[0],) + sink.shape[1:])
    source = gather_directly(picked, "slab", 2)
    stacked = jnp.concatenate([sink[..., :nev], sink[..., nev:]], axis=2)
    prod = jnp.einsum(
        "tmra,tsqab->mtsqrb", stacked, perambulator, preferred_element_type=jnp.float32
    )
    creal = prod[..., :rows, :nev] - prod[..., rows:, nev:]
    cimag = prod[..., :rows, nev:] + prod[..., rows:, :nev]
    half = jnp.concatenate([creal, cimag], axis=4).astype(jnp.bfloat16)
    both = jnp.concatenate([source[..., :nev], source[..., nev:]], axis=2)
    quad = jnp.einsum("mtsqrb,smcb->mtsqrc", half, both, preferred_element_type=jnp.float32)
    dreal = quad[..., :rows, :nev] + quad[..., rows:, nev:]
    dimag = quad[..., rows:, :nev] - quad[..., :rows, nev:]
    return jnp.concatenate([dreal, dimag], axis=-1)


def solution(mesh):
    placed = (P("snk", ("src", "slab"), None), P("snk", "src", None, None, None), P(), P("src"))
    return jax.shard_map(
        local,
        mesh=mesh,
        in_specs=placed,
        out_specs=P(None, "snk", "src", None, "slab", None),
        check_vma=False,
    )
```

profile of v0, /device:TPU:1, one launch (start us, length us, event | category | flops | bytes accessed | tf_op | source)
XLA Modules:
  0.0 182.7 jit_solution(6894072755883903517)
XLA Ops:
  6.5 0.0 copy-start
  6.5 0.0 reduce-scatter.2.cloned.1.call-start
  6.5 1.1 slice_reduce_fusion.2
  7.6 0.1 fusion.59
  7.8 0.5 slice_cosine_fusion.3
  8.2 0.0 copy-start.1
  8.2 4.2 %fusion.6 = (bf16[2,1024,192]{2,1,0:T(8,128)(2,1)S(1)}, bf16[2,1024,192]{2,1,0:T(8,128)(2,1)S(1)}, bf16[2,1024,192]{2,1,0:T(8,128)(2,1)S(1)}, bf16[2,1024,192]{2...) fusion(f32[1024]{0:T(1024)S(1)} %bitcast.69, f32[1024]{0:T(1024)S(1)} %bitcast.68, ...), kind=kLoop, calls=%fused_computation.24 | loop fusion | flops 10223616 | bytes 6316032 | tf_op jit(solution)/shard_map/convert.9
  12.4 0.0 copy-done.1
  12.5 1.2 fusion.40
  13.6 0.3 slice_add_fusion.2
  13.9 1.2 fusion.43
  15.1 0.3 slice_add_fusion.3
  15.4 1.0 fusion.10
  16.4 1.2 fusion.46
  17.5 0.3 slice_add_fusion.4
  17.8 1.2 fusion.49
  19.0 0.3 slice_add_fusion.5
  19.3 0.2 maximum_bitcast_fusion.5
  19.5 0.2 maximum_bitcast_fusion.4
  19.6 0.2 maximum_bitcast_fusion.3
  19.8 0.2 maximum_bitcast_fusion.2
  20.0 1.6 pad_maximum_fusion
  21.5 0.0 reduce-scatter.2.cloned.1.call-update
  21.6 0.0 copy-start.3
  21.6 43.2 %reduce-scatter.2.cloned.1.call-done = f32[2,4,24,384]{3,2,0,1:T(8,128)} async-done(((f32[2,4,192,384]{3,2,0,1:T(8,128)}), f32[2,4,24,384]{3,2,0,1:T(8,128)}) %reduce-scatter.2.cloned.1.call-update) | async-done | bytes 294928 | tf_op jit(solution)/shard_map/reduce_scatter | solution.py:78
  64.8 1.1 copy.57
  65.9 0.7 copy.58
  66.6 4.1 %all-to-all-start = ((f32[4,2,4,6,384]{4,2,3,1,0:T(4,128)}), f32[4,2,4,6,384]{4,2,3,1,0:T(4,128)S(1)}, u32[]{:S(2)}, u32[]{:S(2)}) async-start(f32[4,2,4,6,384]{4,2,3,1,0:T(4,128)} %copy.58), calls=%async_computation.1 | async-start | bytes 589824 | tf_op jit(solution)/shard_map/all_to_all | solution.py:21
  70.8 5.7 %all-to-all-done = f32[4,2,4,6,384]{4,2,3,1,0:T(4,128)S(1)} async-done(((f32[4,2,4,6,384]{4,2,3,1,0:T(4,128)}), f32[4,2,4,6,384]{4,2,3,1,0:T(4,128)S(1)}, u32[]{:S(2)}, u32[]{:S(2)}) %all-to-all-start) | async-done | bytes 294944 | tf_op jit(solution)/shard_map/all_to_all | solution.py:21
  76.5 0.1 reduce_sum.21
  76.6 0.7 broadcast_in_dim.6
  77.3 3.3 %all-to-all-start.1 = ((bf16[4,2,4,6,384]{4,2,3,1,0:T(4,128)(2,1)}), bf16[4,2,4,6,384]{4,2,3,1,0:T(4,128)(2,1)S(1)}, u32[]{:S(2)}, u32[]{:S(2)}) async-start(bf16[4,2,4,6,384]{4,2,3,1,0:T(4,128)(2,1)} %broadcast_in_dim.6), calls=%async_computation.2 | async-start | bytes 294912 | tf_op jit(solution)/shard_map/all_to_all | solution.py:33
  80.6 4.9 %all-to-all-done.1 = bf16[4,2,4,6,384]{4,2,3,1,0:T(4,128)(2,1)S(1)} async-done(((bf16[4,2,4,6,384]{4,2,3,1,0:T(4,128)(2,1)}), bf16[4,2,4,6,384]{4,2,3,1,0:T(4,128)(2,1)S(1)}, u32[]{:S(2)}, u32[]{:S(2)}) %all-to-all-start.1) | async-done | bytes 147488 | tf_op jit(solution)/shard_map/all_to_all | solution.py:33
  85.5 0.0 copy-start.2
  85.5 0.1 reshape_reshape.3
  85.6 0.0 copy-done.3
  85.6 0.4 convolution_convert_fusion
  86.0 0.1 copy-done.2
  86.1 0.6 broadcast_in_dim.7
  86.7 24.1 %all_to_all.20 = bf16[8,2,36864]{2,1,0:T(2,128)(2,1)S(1)} all-to-all(bf16[8,2,36864]{2,1,0:T(2,128)(2,1)S(1)} %broadcast_in_dim.7), channel_id=1, replica_groups=mesh['src'=4,'snk'=8,'slab'=8] {'snk'}, dimensions={0} | all-to-all | bytes 2359296 | tf_op jit(solution)/shard_map/all_to_all | solution.py:33
  110.8 2.0 %reduce_sum.22 = bf16[2,36864]{1,0:T(2,128)(2,1)} reduce(bf16[8,2,36864]{2,1,0:T(2,128)(2,1)S(1)} %all_to_all.20, bf16[]{:T(256)} %constant.93.clone.1), dimensions={0}, to_apply=%region_2.3 | reduce | flops 516096 | bytes 1327106 | tf_op jit(solution)/shard_map/reduce_sum | solution.py:41
  112.8 0.9 copy.81
  113.7 1.1 broadcast_in_dim.8
  114.9 21.6 %all-to-all-start.3 = ((bf16[8,2,4,24,384]{4,3,2,1,0:T(8,128)(2,1)}), bf16[8,2,4,24,384]{4,3,2,1,0:T(8,128)(2,1)S(1)}, u32[]{:S(2)}, u32[]{:S(2)}) async-start(bf16[8,2,4,24,384]{4,3,2,1,0:T(8,128)(2,1)} %broadcast_in_dim.8), calls=%async_computation.4 | async-start | bytes 2359296 | tf_op jit(solution)/shard_map/all_to_all | solution.py:33
  136.4 1.0 copy.64
  137.4 0.1 fusion.84
  137.6 0.0 copy-done
  137.6 0.8 fusion.2
  138.4 2.1 %fusion.22 = (bf16[4,2,2,4,24,192]{5,4,3,2,0,1:T(8,128)(2,1)}, bf16[4,2,2,4,24,192]{5,4,3,2,0,1:T(8,128)(2,1)}) fusion(f32[4,2,2,4,48,384]{5,4,3,2,0,1:T(8,128)S(1)} %fusion.2), kind=kLoop, calls=%fused_computation.44 | loop fusion | flops 1179648 | bytes 5898240 | tf_op jit(solution)/shard_map/convert.1
  140.4 24.6 %all-to-all-done.3 = bf16[8,2,4,24,384]{4,3,2,1,0:T(8,128)(2,1)S(1)} async-done(((bf16[8,2,4,24,384]{4,3,2,1,0:T(8,128)(2,1)}), bf16[8,2,4,24,384]{4,3,2,1,0:T(8,128)(2,1)S(1)}, u32[]{:S(2)}, u32[]{:S(2)}) %all-to-all-start.3) | async-done | bytes 1179680 | tf_op jit(solution)/shard_map/all_to_all | solution.py:33
  165.0 0.2 copy.61
  165.2 1.3 fusion.83
  166.4 2.4 %copy.78 = bf16[2,4,192,192]{2,3,0,1:T(8,128)(2,1)} copy(bf16[2,4,192,192]{3,2,1,0:T(8,128)(2,1)} %get-tuple-element.25) | data formatting | bytes 1179648
  168.8 1.2 copy.77
  170.0 2.9 %convolution_bitcast_fusion = f32[4,2,2,4,48,384]{5,4,3,1,2,0:T(8,128)S(1)} fusion(bf16[2,4,192,192]{2,3,0,1:T(8,128)(2,1)} %copy.78, bf16[2,4,192,192]{2,3,0,1:T(8,128)(2,1)} %copy.77, bf16[4,2,2,4,24,192]{5,4,3,2,0,1:T(8,128)(2,1)} %get-tuple-element.11, bf16[4,2,2,4,24,192]{5,4,3,2,0,1:T(8,128)(2,1)} %get-tuple-element.10), kind=kOutput, calls=%fused_computation.22 | convolution fusion | flops 457703424 | bytes 7077888 | tf_op jit(solution)/shard_map/mtsqrb,smcb->mtsqrc/dot_general | solution.py:94
  172.9 0.9 slice_add_fusion
  173.8 0.5 pad_maximum_fusion.1
  174.3 1.6 copy.68
  (6 shorter events, 0.1 us)
Async XLA Ops:
  6.5 131.1 %copy-start = (bf16[2,2,4,192,384]{4,3,2,1,0:T(8,128)(2,1)S(1)}, bf16[2,2,4,192,384]{4,3,2,1,0:T(8,128)(2,1)}, u32[]{:S(2)}) copy-start(bf16[2,2,4,192,384]{4,3,2,1,0:T(8,128)(2,1)} %param.5) | copy-start | bytes 7077892
  6.5 58.3 %reduce-scatter.2.cloned.1.call-start = ((), (), s32[]{:S(2)}) async-start(), calls=%async_computation.5 | async-start | bytes 2654208 | tf_op jit(solution)/shard_map/reduce_scatter | solution.py:78
  8.2 4.2 %copy-start.1 = (bf16[2,1024,384]{2,1,0:T(8,128)(2,1)S(1)}, bf16[2,1024,384]{2,1,0:T(8,128)(2,1)}, u32[]{:S(2)}) copy-start(bf16[2,1024,384]{2,1,0:T(8,128)(2,1)} %param.4) | copy-start | bytes 4718596
  21.6 64.1 %copy-start.3 = (s32[2]{0:T(128)S(1)}, s32[2]{0:T(128)}, u32[]{:S(2)}) copy-start(s32[2]{0:T(128)} %param.7) | copy-start | bytes 28
  66.6 9.9 %all-to-all-start = ((f32[4,2,4,6,384]{4,2,3,1,0:T(4,128)}), f32[4,2,4,6,384]{4,2,3,1,0:T(4,128)S(1)}, u32[]{:S(2)}, u32[]{:S(2)}) async-start(f32[4,2,4,6,384]{4,2,3,1,0:T(4,128)} %copy.58), calls=%async_computation.1 | async-start | bytes 589824 | tf_op jit(solution)/shard_map/all_to_all | solution.py:21
  77.3 8.2 %all-to-all-start.1 = ((bf16[4,2,4,6,384]{4,2,3,1,0:T(4,128)(2,1)}), bf16[4,2,4,6,384]{4,2,3,1,0:T(4,128)(2,1)S(1)}, u32[]{:S(2)}, u32[]{:S(2)}) async-start(bf16[4,2,4,6,384]{4,2,3,1,0:T(4,128)(2,1)} %broadcast_in_dim.6), calls=%async_computation.2 | async-start | bytes 294912 | tf_op jit(solution)/shard_map/all_to_all | solution.py:33
  85.5 0.7 copy-start.2
  114.9 50.1 %all-to-all-start.3 = ((bf16[8,2,4,24,384]{4,3,2,1,0:T(8,128)(2,1)}), bf16[8,2,4,24,384]{4,3,2,1,0:T(8,128)(2,1)S(1)}, u32[]{:S(2)}, u32[]{:S(2)}) async-start(bf16[8,2,4,24,384]{4,3,2,1,0:T(8,128)(2,1)} %broadcast_in_dim.8), calls=%async_computation.4 | async-start | bytes 2359296 | tf_op jit(solution)/shard_map/all_to_all | solution.py:33
Sparse Core Ops, SparseCore 0:
  21.7 43.0 reduce-scatter.1
where the time goes:
time: 183 us
  waiting for transfers between devices  78.4 us (43%)
  starting transfers between devices  29.1 us (16%)
  blocking collectives  24.1 us (13%)
  local copies, waits for them, and re-layouts  14.7 us (8%)
  other arithmetic  14.2 us (8%)
  between operations  13.6 us (7%)
  matrix products  8.7 us (5%)
    reduce_scatter x1, waiting for transfers between devices, local(): lax.psum_scatter(partial_value, 'slab', scatter_dimension=2, tiled=True)  43.2 us
    all_to_all x2, waiting for transfers between devices, copy_for_each(): return lax.all_to_all(copies, axis, split_axis=0, concat_axis=0, tiled=True)  29.4 us
    all_to_all x2, starting transfers between devices, copy_for_each(): return lax.all_to_all(copies, axis, split_axis=0, concat_axis=0, tiled=True)  24.9 us
    all_to_all x1, blocking collectives, copy_for_each(): return lax.all_to_all(copies, axis, split_axis=0, concat_axis=0, tiled=True)  24.1 us
    another operation x3, other arithmetic  7.25 us
    all_to_all x1, waiting for transfers between devices, summed_on_arrival(): lax.all_to_all(parts, axis, split_axis=0, concat_axis=0, tiled=True)  5.7 us
    unnamed x13, local copies, waits for them, and re-layouts  4.69 us
    dot_general x4, matrix products, local(): jnp.einsum('tsa,tsb->tab', eigvecs, phased, preferred_element_type=jnp.fl...  4.68 us
  transfers between devices with their start and end apart: 4, of which 4 were waited for; matrix products, arithmetic and copies ran while one was open for 2% of the time, Pallas kernels for 0%

commit v1 on v0

v1 whole, which is shorter than its diff:
```python
import math

import jax
import jax.numpy as jnp
from jax import lax
from jax.experimental import pallas as pl
from jax.experimental.pallas import tpu as pltpu
from jax.sharding import PartitionSpec as P

LX = 32
LY = 32
ZPL = 1
NX = 4
NY = 4
NZ = 8
ZLO = 4
MESH = pl.DeviceIdType.MESH
F32 = jnp.float32
BF16 = jnp.bfloat16


def angles(momenta, xs, ys, zs, lz):
    fx = (momenta[:, 0:1] * xs[None, :] % LX).astype(jnp.float32) / LX
    fy = (momenta[:, 1:2] * ys[None, :] % LY).astype(jnp.float32) / LY
    fz = (momenta[:, 2:3] * zs[None, :] % lz).astype(jnp.float32) / lz
    return 2.0 * math.pi * (fx + fy + fz)


def block_of(z):
    return lax.rem(z, ZLO) * 2 + lax.div(z, ZLO)


def exchange(part, st, sink, src, d2d, ysend, yrecv, q, zrecv, xall, stall, sel, srecv,
             d2d_s, d2d_r, st_s, st_r, y_s, y_r, z_s, z_r, x_s, x_r, sink_s, sink_r, sel_s, sel_r,
             ring_s, ring_r, sib_s, sib_r):
    y = lax.axis_index("src")
    snk = lax.axis_index("snk")
    slab = lax.axis_index("slab")
    zh, x = lax.div(snk, NX), lax.rem(snk, NX)
    zl, c = lax.div(slab, 2), lax.rem(slab, 2)
    z = zh * ZLO + zl
    own = block_of(z)

    def at(y=y, x=x, z=None, zh=zh, zl=zl, c=c):
        if z is not None:
            zh, zl = lax.div(z, ZLO), lax.rem(z, ZLO)
        return {"src": y, "snk": zh * NX + x, "slab": zl * 2 + c}

    def turn(value, by, size):
        return lax.rem(value + by, size)

    def copy(source, target, send, recv, device):
        return pltpu.make_async_remote_copy(
            src_ref=source, dst_ref=target, send_sem=send, recv_sem=recv, device_id=device, device_id_type=MESH
        )

    barrier = pltpu.get_barrier_semaphore()
    peers = [at(y=turn(y, k // 4, NY), zh=turn(zh, k // 2 % 2, 2), c=turn(c, k % 2, 2)) for k in range(1, 16)]
    peers += [at(z=turn(z, k, NZ)) for k in (1, 2, 3, 5, 6, 7)]
    peers += [at(x=turn(x, k, NX)) for k in (1, 2, 3)]
    for peer in peers:
        pl.semaphore_signal(barrier, inc=1, device_id=peer, device_id_type=MESH)
    pl.semaphore_wait(barrier, len(peers))

    sends = []
    sibling = at(c=1 - c)

    pair = {}
    for d in (1, 3, 2, 0):
        pair[d] = copy(part.at[1 - c, turn(y, d, NY)], d2d.at[d], d2d_s.at[d], d2d_r.at[d], sibling)
        pair[d].start()
        sends.append(pair[d])
    stall[y] = st[...]
    times = []
    for d in (1, 2, 3):
        times.append(copy(stall.at[y], stall.at[y], st_s.at[d - 1], st_r.at[turn(y, 0, NY)], at(y=turn(y, d, NY))))
        times[-1].start()
    sends += times

    along = []
    for d in (1, 3, 2):
        pair[d].wait_recv()
        ysend[d - 1] = (part[c, turn(y, d, NY)].astype(F32) + d2d[d].astype(F32)).astype(BF16)
        along.append(copy(ysend.at[d - 1], yrecv.at[d - 1], y_s.at[d - 1], y_r.at[d - 1], at(y=turn(y, d, NY))))
        along[-1].start()
    sends += along
    pair[0].wait_recv()
    for each in along:
        each.wait_recv()

    def summed(block):
        total = part[c, y, block].astype(F32) + d2d[0, block].astype(F32)
        for d in range(3):
            total += yrecv[d, block].astype(F32)
        return total.astype(BF16)

    for dz in (4, 3, 5, 2, 6, 1, 7):
        to = turn(z, dz, NZ)
        q[dz] = summed(block_of(to))
        each = copy(q.at[dz], zrecv.at[z], z_s.at[dz], z_r.at[z], at(z=to))
        each.start()
        sends.append(each)
    zrecv[z] = summed(own)
    for dz in range(1, NZ):
        come = turn(z, dz, NZ)
        copy(q.at[dz], zrecv.at[come], z_s.at[dz], z_r.at[come], at(z=come)).wait_recv()
    for g in range(2):
        total = zrecv[g * ZLO].astype(F32)
        for k in range(1, ZLO):
            total += zrecv[g * ZLO + k].astype(F32)
        xall[x, g] = total.astype(BF16)

    across = []
    for d in (1, 3, 2):
        across.append(copy(xall.at[x], xall.at[x], x_s.at[d - 1], x_r.at[x], at(x=turn(x, d, NX))))
        across[-1].start()
    sends += across

    for dy, dg in ((1, 0), (3, 0), (2, 0), (0, 1), (1, 1), (3, 1), (2, 1)):
        g = turn(zh, dg, 2)
        each = copy(xall.at[x, g], sink.at[c, y], sink_s.at[dy, dg], sink_r.at[c, y],
                    at(y=turn(y, dy, NY), zh=g, c=zh))
        each.start()
        sends.append(each)
    to_sibling = copy(xall.at[x, zh], sink.at[c, y], sink_s.at[0, 0], sink_r.at[c, y], sibling)

    @pl.when(c == zh)
    def _():
        sink[c, y] = xall[x, zh]

    @pl.when(c != zh)
    def _():
        to_sibling.start()

    for d in (1, 2, 3):
        come = turn(x, d, NX)
        copy(xall.at[come], xall.at[come], x_s.at[d - 1], x_r.at[come], at(x=come)).wait_recv()
    for d in (1, 2, 3):
        come = turn(y, d, NY)
        copy(stall.at[come], stall.at[come], st_s.at[d - 1], st_r.at[come], at(y=come)).wait_recv()

    def picked(plane, s):
        wanted = stall[plane, s][0:1]
        total = jnp.zeros((24, 384), F32)
        for k in range(NX):
            for g in range(2):
                total += jnp.where(wanted == 2 * (g * NX + k) + c, xall[k, g].astype(F32), 0.0)
        return total.astype(BF16)

    for dy, ds in ((1, 0), (1, 1), (3, 0), (3, 1), (2, 0), (2, 1), (0, 1)):
        plane, s = turn(y, dy, NY), turn(c, ds, 2)
        sel[dy, ds] = picked(plane, s)
        each = copy(sel.at[dy, ds], srecv.at[y, c], sel_s.at[dy, ds], sel_r.at[y, c], at(y=plane, c=s))
        each.start()
        sends.append(each)
    srecv[y, c] = picked(y, c)
    for dy, ds in ((1, 0), (1, 1), (3, 0), (3, 1), (2, 0), (2, 1), (0, 1)):
        m, k = turn(y, dy, NY), turn(c, ds, 2)
        copy(sel.at[dy, ds], srecv.at[m, k], sel_s.at[dy, ds], sel_r.at[m, k], at(y=m, c=k)).wait_recv()
    for m in range(NY):
        src[c, m, own] = srecv[m, 0] + srecv[m, 1]

    def rows(height, p):
        return src.at[c, pl.ds(2 * p, 2), block_of(height)]

    def hop(way, k, p):
        held = turn(z, NZ - (k - 1) if way == 0 else k - 1, NZ)
        to = turn(z, 1 if way == 0 else NZ - 1, NZ)
        return copy(rows(held, p), rows(held, p), ring_s.at[way, k - 1, p], ring_r.at[way, k - 1, p], at(z=to))

    def come(way, k, p):
        held = turn(z, NZ - k if way == 0 else k, NZ)
        to = turn(z, 1 if way == 0 else NZ - 1, NZ)
        copy(rows(held, p), rows(held, p), ring_s.at[way, k - 1, p], ring_r.at[way, k - 1, p], at(z=to)).wait_recv()

    siblings = []

    def share(slot, height, p):
        each = copy(rows(height, p), rows(height, p), sib_s.at[slot, p], sib_r.at[slot, p], sibling)
        each.start()
        sends.append(each)
        other = src.at[1 - c, pl.ds(2 * p, 2), block_of(height)]
        siblings.append(copy(other, other, sib_s.at[slot, p], sib_r.at[slot, p], sibling))

    def go(way, k, p):
        each = hop(way, k, p)
        each.start()
        sends.append(each)

    for p in range(2):
        go(0, 1, p)
        go(1, 1, p)
    for p in range(2):
        share(0, z, p)
    for k in (1, 2, 3):
        for p in range(2):
            for way in range(2):
                come(way, k, p)
                if k < 3 or p == way:
                    go(way, k + 1, p)
                share(k + 3 * way, turn(z, NZ - k if way == 0 else k, NZ), p)
    for way in range(2):
        come(way, 4, way)
        share(7, turn(z, 4, NZ), way)

    for each in siblings:
        each.wait_recv()
    for dy in range(NY):
        for dc in range(2):
            m, k = turn(y, dy, NY), turn(c, dc, 2)
            piece = copy(xall.at[x, 0], sink.at[k, m], sink_s.at[dy, dc], sink_r.at[k, m], at(y=m))
            if dy or dc:
                piece.wait_recv()
            else:
                pl.when(c != zh)(piece.wait_recv)
    for each in sends:
        each.wait_send()
    pl.when(c != zh)(to_sibling.wait_send)


def exchanged(part, st):
    dma = pltpu.SemaphoreType.DMA
    rows = (24, 384)

    def vmem(*lead):
        return pltpu.VMEM(lead + rows, BF16)

    whole = pl.BlockSpec(memory_space=pltpu.VMEM)
    return pl.pallas_call(
        exchange,
        out_shape=(jax.ShapeDtypeStruct((2, 4) + rows, BF16), jax.ShapeDtypeStruct((2, 4, 8) + rows, BF16)),
        in_specs=[whole, whole],
        out_specs=(whole, whole),
        scratch_shapes=[
            vmem(4, 8), vmem(3, 8), vmem(3, 8), vmem(8), vmem(8), vmem(4, 2), pltpu.VMEM((4, 2, 8, 384), jnp.int32),
            vmem(4, 2), vmem(4, 2),
            dma((4,)), dma((4,)), dma((3,)), dma((4,)), dma((3,)), dma((3,)), dma((8,)), dma((8,)),
            dma((3,)), dma((4,)), dma((4, 2)), dma((2, 4)), dma((4, 2)), dma((4, 2)),
            dma((2, 4, 2)), dma((2, 4, 2)), dma((8, 2)), dma((8, 2)),
        ],
        compiler_params=pltpu.CompilerParams(
            collective_id=0, has_side_effects=True, vmem_limit_bytes=48 * 1024 * 1024
        ),
    )(part, st)


def local(eigvecs, perambulator, momenta, source_times):
    nev = eigvecs.shape[2] // 2
    count = eigvecs.shape[1]
    slabs = lax.axis_size("slab")
    lz = ZPL * lax.axis_size("src") * slabs
    sites = jnp.arange(count, dtype=jnp.int32)
    xs = sites % LX
    ys = sites // LX % LY
    zs = sites // (LX * LY) + lax.axis_index(("src", "slab")) * ZPL
    angle = angles(momenta, xs, ys, zs, lz)
    vreal = eigvecs[:, :, :nev].astype(jnp.float32)
    vimag = eigvecs[:, :, nev:].astype(jnp.float32)
    partials = []
    for m in range(angle.shape[0]):
        cosine = jnp.cos(angle[m])[None, :, None]
        sine = jnp.sin(angle[m])[None, :, None]
        phased = jnp.concatenate(
            [cosine * vreal + sine * vimag, cosine * vimag - sine * vreal], axis=2
        ).astype(jnp.bfloat16)
        gram = jnp.einsum("tsa,tsb->tab", eigvecs, phased, preferred_element_type=jnp.float32)
        real = gram[:, :nev, :nev] + gram[:, nev:, nev:]
        imag = gram[:, :nev, nev:] - gram[:, nev:, :nev]
        partials.append(jnp.concatenate([real, imag], axis=2))
    part = jnp.stack(partials, axis=1).astype(jnp.bfloat16).reshape(2, 4, 8, 24, 384)
    st = jnp.broadcast_to(source_times[:, None, None], (2, 8, 384))
    sink, source = exchanged(part, st)
    rows = nev // slabs
    source = source.reshape(2, 4, nev, 2 * nev)
    stacked = jnp.concatenate([sink[..., :nev], sink[..., nev:]], axis=2)
    prod = jnp.einsum(
        "tmra,tsqab->mtsqrb", stacked, perambulator, preferred_element_type=jnp.float32
    )
    creal = prod[..., :rows, :nev] - prod[..., rows:, nev:]
    cimag = prod[..., :rows, nev:] + prod[..., rows:, :nev]
    half = jnp.concatenate([creal, cimag], axis=4).astype(jnp.bfloat16)
    both = jnp.concatenate([source[..., :nev], source[..., nev:]], axis=2)
    quad = jnp.einsum("mtsqrb,smcb->mtsqrc", half, both, preferred_element_type=jnp.float32)
    dreal = quad[..., :rows, :nev] + quad[..., rows:, nev:]
    dimag = quad[..., rows:, :nev] - quad[..., :rows, nev:]
    return jnp.concatenate([dreal, dimag], axis=-1)


def solution(mesh):
    placed = (P("snk", ("src", "slab"), None), P("snk", "src", None, None, None), P(), P("src"))
    return jax.shard_map(
        local,
        mesh=mesh,
        in_specs=placed,
        out_specs=P(None, "snk", "src", None, "slab", None),
        check_vma=False,
    )
```

time: 183 us -> 78.4 us (0.43)
  waiting for transfers between devices: 78.4 us -> 0 us
  Pallas kernels: 0 us -> 52.5 us
  starting transfers between devices: 29.1 us -> 0 us
  blocking collectives: 24.1 us -> 0 us
  between operations: 13.6 us -> 0.16 us
  local copies, waits for them, and re-layouts: 14.7 us -> 9.25 us
  other arithmetic: 14.2 us -> 9.8 us
  matrix products: 8.7 us -> 6.49 us
    pallas_call x0 -> x1, Pallas kernels: none -> 52.5 us  [exchanged(): pl.pallas_call(exchange, out_shape=(jax.ShapeDtypeStruct((2, 4) + rows, B...]
    reduce_scatter x1 -> x0, waiting for transfers between devices: 43.2 us -> none  [local(): lax.psum_scatter(partial_value, 'slab', scatter_dimension=2, tiled=True)]
    all_to_all x3 -> x0, waiting for transfers between devices: 35.1 us -> none  [the longest x2 29.4 us: copy_for_each(): return lax.all_to_all(copies, axis, split_axis=0, concat_axis=0, tiled=True)]
    all_to_all x3 -> x0, starting transfers between devices: 29 us -> none  [the longest x2 24.9 us: copy_for_each(): return lax.all_to_all(copies, axis, split_axis=0, concat_axis=0, tiled=True)]
    all_to_all x1 -> x0, blocking collectives: 24.1 us -> none  [copy_for_each(): return lax.all_to_all(copies, axis, split_axis=0, concat_axis=0, tiled=True)]
    reduce_sum x2 -> x0, other arithmetic: 2.06 us -> none  [the longest x1 2 us: over_copies(): return copy_for_each(shard, axis).astype(jnp.float32).sum(axis=0)]
    dot_general x1, matrix products: 2.89 us -> 1.04 us  [local(): jnp.einsum('mtsqrb,smcb->mtsqrc', half, both, preferred_element_type=jnp....]
    unnamed x13 -> x10, local copies, waits for them, and re-layouts: 4.69 us -> 4.06 us
  transfers between devices with their start and end apart: 4 -> 0, of which waited for: 4 -> 0; matrix products, arithmetic and copies ran while one was open for 2% -> 0% of each run, Pallas kernels for 0% -> 0%
where the time goes in v1:
time: 78.4 us; the launch traced here: 78.2 us
  Pallas kernels  52.5 us (67%)
  other arithmetic  9.8 us (12%)
  local copies, waits for them, and re-layouts  9.25 us (12%)
  matrix products  6.49 us (8%)
    pallas_call x1, Pallas kernels, exchanged(): pl.pallas_call(exchange, out_shape=(jax.ShapeDtypeStruct((2, 4) + rows, B...  52.5 us
    another operation x7, other arithmetic  7.63 us
    dot_general x4, matrix products, local(): jnp.einsum('tsa,tsb->tab', eigvecs, phased, preferred_element_type=jnp.fl...  4.68 us
    unnamed x10, local copies, waits for them, and re-layouts  4.06 us
    concatenate x1, local copies, waits for them, and re-layouts, local(): return jnp.concatenate([dreal, dimag], axis=-1)  1.59 us

profile of v1, /device:TPU:1, one launch (start us, length us, event | category | flops | bytes accessed | tf_op | source)
XLA Modules:
  0.0 78.2 jit_solution(4724003658579493464)
XLA Ops:
  0.0 0.0 copy-start
  0.0 1.1 %slice_reduce_fusion.2 = (s32[4]{0:T(128)S(1)}, s32[4]{0:T(128)S(1)}, s32[4]{0:T(128)S(1)}) fusion(s32[4,3]{1,0:T(4,128)} %param.6), kind=kLoop, calls=%fused_computation.146 | loop fusion | bytes 96 | tf_op jit(solution)/shard_map/slice | solution.py:23
  1.1 0.1 fusion.67
  1.2 0.5 slice_cosine_fusion.3
  1.7 0.7 broadcast_in_dim.2.st
  2.4 0.0 copy-start.1
  2.4 2.7 %fusion.10 = (bf16[2,1024,192]{2,1,0:T(8,128)(2,1)S(1)}, bf16[2,1024,192]{2,1,0:T(8,128)(2,1)S(1)}) fusion(f32[1024]{0:T(1024)S(1)} %bitcast.57, f32[1024]{0:T(1024)S(1)} %bitcast.58, bf16[2,1024,384]{2,1,0:T(8,128)(2,1)} %param.4), kind=kLoop, calls=%fused_computation.26 | loop fusion | flops 3932160 | bytes 3153920 | tf_op jit(solution)/shard_map/convert.22
  5.1 0.0 copy-done.1
  5.1 1.2 %fusion.46 = f32[2,384,384]{2,1,0:T(8,128)S(1)} fusion(bf16[2,1024,384]{2,1,0:T(8,128)(2,1)S(1)} %copy-done.1, bf16[2,1024,192]{2,1,0:T(8,128)(2,1)S(1)} %get-tuple-element.19, bf16[2,1024,192]{2,1,0:T(8,128)(2,1)S(1)} %get-tuple-element.18), kind=kOutput, calls=%fused_computation.63 | convolution fusion | flops 607125504 | bytes 4325376 | tf_op jit(solution)/shard_map/tsa,tsb->tab/dot_general | solution.py:266
  6.3 0.3 fusion.59
  6.6 0.1 pad_maximum_fusion.4
  6.7 3.0 %fusion.6 = (bf16[2,1024,192]{2,1,0:T(8,128)(2,1)S(1)}, bf16[2,1024,192]{2,1,0:T(8,128)(2,1)S(1)}, bf16[2,1024,192]{2,1,0:T(8,128)(2,1)S(1)}, bf16[2,1024,192]{2...) fusion(f32[1024]{0:T(1024)S(1)} %bitcast.52, f32[1024]{0:T(1024)S(1)} %bitcast.51, ...), kind=kLoop, calls=%fused_computation.22 | loop fusion | flops 10223616 | bytes 6316032 | tf_op jit(solution)/shard_map/convert.24
  9.7 1.2 %fusion.49 = f32[2,384,384]{2,1,0:T(8,128)S(1)} fusion(bf16[2,1024,384]{2,1,0:T(8,128)(2,1)S(1)} %copy-done.1, bf16[2,1024,192]{2,1,0:T(8,128)(2,1)S(1)} %get-tuple-element.17, bf16[2,1024,192]{2,1,0:T(8,128)(2,1)S(1)} %get-tuple-element.16), kind=kOutput, calls=%fused_computation.64 | convolution fusion | flops 607125504 | bytes 4325376 | tf_op jit(solution)/shard_map/tsa,tsb->tab/dot_general | solution.py:266
  10.9 0.3 fusion.61
  11.1 0.1 pad_maximum_fusion.3
  11.3 1.2 %fusion.40 = f32[2,384,384]{2,1,0:T(8,128)S(1)} fusion(bf16[2,1024,384]{2,1,0:T(8,128)(2,1)S(1)} %copy-done.1, bf16[2,1024,192]{2,1,0:T(8,128)(2,1)S(1)} %get-tuple-element.24, bf16[2,1024,192]{2,1,0:T(8,128)(2,1)S(1)} %get-tuple-element.25), kind=kOutput, calls=%fused_computation.61 | convolution fusion | flops 607125504 | bytes 4325376 | tf_op jit(solution)/shard_map/tsa,tsb->tab/dot_general | solution.py:266
  12.4 1.2 %fusion.43 = f32[2,384,384]{2,1,0:T(8,128)S(1)} fusion(bf16[2,1024,384]{2,1,0:T(8,128)(2,1)S(1)} %copy-done.1, bf16[2,1024,192]{2,1,0:T(8,128)(2,1)S(1)} %get-tuple-element.26, bf16[2,1024,192]{2,1,0:T(8,128)(2,1)S(1)} %get-tuple-element.27), kind=kOutput, calls=%fused_computation.62 | convolution fusion | flops 607125504 | bytes 4325376 | tf_op jit(solution)/shard_map/tsa,tsb->tab/dot_general | solution.py:266
  13.6 0.3 fusion.57
  13.9 0.3 fusion.55
  14.2 0.1 pad_maximum_fusion.6
  14.3 0.1 pad_maximum_fusion.5
  14.4 0.2 pad_maximum_fusion.2.part
  14.6 52.5 %shard_map.46 = (bf16[2,4,24,384]{3,2,1,0:T(8,128)(2,1)S(1)}, bf16[2,4,8,24,384]{4,3,2,1,0:T(8,128)(2,1)S(1)}) custom-call(bf16[2,4,8,24,384]{4,3,2,1,0:T(8,128)(2,1)S(1)} %pad_maximum_fusion.2.part, s32[2,8,384]{2,1,0:T(8,128)S(1)} %broadcast_in_dim.2.st), custom_call_target="tpu_custom_call" | custom-call | tf_op jit(solution)/shard_map/pallas_call | solution.py:229
  67.2 0.1 fusion.89
  67.3 1.2 %fusion.88 = (bf16[2,4,192,192]{3,2,1,0:T(8,128)(2,1)}, bf16[2,4,192,192]{3,2,1,0:T(8,128)(2,1)S(1)}) fusion(bf16[2,4,192,384]{3,2,1,0:T(8,128)(2,1)S(1)} %bitcast.46), kind=kLoop, calls=%fused_computation.153 | loop fusion | bytes 2359296 | tf_op jit(solution)/shard_map/slice | solution.py:282
  68.5 2.4 %copy.20 = bf16[2,4,192,192]{2,3,0,1:T(8,128)(2,1)} copy(bf16[2,4,192,192]{3,2,1,0:T(8,128)(2,1)} %get-tuple-element.28) | data formatting | bytes 1179648
  70.9 1.2 %copy.21 = bf16[2,4,192,192]{2,3,0,1:T(8,128)(2,1)} copy(bf16[2,4,192,192]{3,2,1,0:T(8,128)(2,1)S(1)} %get-tuple-element.29) | data formatting | bytes 1179648
  72.1 0.0 copy-done
  72.1 0.8 fusion.2
  72.9 0.0 copy-start.2
  72.9 0.0 copy-start.3
  72.9 0.9 %fusion.22 = (bf16[4,2,2,4,24,192]{5,4,3,2,0,1:T(8,128)(2,1)S(1)}, bf16[4,2,2,4,24,192]{5,4,3,2,0,1:T(8,128)(2,1)S(1)}) fusion(f32[4,2,2,4,48,384]{5,4,3,2,0,1:T(8,128)S(1)} %fusion.2), kind=kLoop, calls=%fused_computation.42 | loop fusion | flops 1179648 | bytes 5898240 | tf_op jit(solution)/shard_map/convert
  73.8 0.2 copy-done.2
  74.0 0.2 copy-done.3
  74.2 1.0 %convolution_bitcast_fusion = f32[4,2,2,4,48,384]{5,4,3,1,2,0:T(8,128)S(1)} fusion(bf16[2,4,192,192]{2,3,0,1:T(8,128)(2,1)S(1)} %copy-done.3, bf16[2,4,192,192]{2,3,0,1:T(8,128)(2,1)S(1)} %copy-done.2, bf16[4,2,2,4,24,192]{5,4,3,2,0,1:T(8,128)(2,1)S(1)} %get-tuple-element.15, bf16[4,2,2,4,24,192]{5,4,3,2,0,1:T(8,128)(2,1)S(1)} %get-tuple-element.14), kind=kOutput, calls=%fused_computation.20 | convolution fusion | flops 457703424 | bytes 7077888 | tf_op jit(solution)/shard_map/mtsqrb,smcb->mtsqrc/dot_general | solution.py:283
  75.3 0.9 %slice_add_fusion = (f32[4,2,2,4,24,192]{5,4,3,1,2,0:T(8,128)S(1)}, f32[4,2,2,4,24,192]{5,4,3,1,2,0:T(8,128)S(1)}) fusion(f32[4,2,2,4,48,384]{5,4,3,1,2,0:T(8,128)S(1)} %convolution_bitcast_fusion), kind=kLoop, calls=%fused_computation.38 | loop fusion | flops 589824 | bytes 7077888 | tf_op jit(solution)/shard_map/add | solution.py:284
  76.2 0.5 pad_maximum_fusion
  76.7 1.6 %copy.12 = f32[4,2,2,4,24,384]{5,4,3,2,1,0:T(8,128)} copy(f32[4,2,2,4,24,384]{5,4,3,1,2,0:T(8,128)S(1)} %pad_maximum_fusion) | data formatting | bytes 4718592 | tf_op jit(solution)/shard_map/concatenate | solution.py:286
  (2 shorter events, 0.0 us)
Async XLA Ops:
  0.0 72.1 %copy-start = (bf16[2,2,4,192,384]{4,3,2,1,0:T(8,128)(2,1)S(1)}, bf16[2,2,4,192,384]{4,3,2,1,0:T(8,128)(2,1)}, u32[]{:S(2)}) copy-start(bf16[2,2,4,192,384]{4,3,2,1,0:T(8,128)(2,1)} %param.5) | copy-start | bytes 7077892
  2.4 2.7 %copy-start.1 = (bf16[2,1024,384]{2,1,0:T(8,128)(2,1)S(1)}, bf16[2,1024,384]{2,1,0:T(8,128)(2,1)}, u32[]{:S(2)}) copy-start(bf16[2,1024,384]{2,1,0:T(8,128)(2,1)} %param.4) | copy-start | bytes 4718596
  72.9 1.1 %copy-start.2 = (bf16[2,4,192,192]{2,3,0,1:T(8,128)(2,1)S(1)}, bf16[2,4,192,192]{2,3,0,1:T(8,128)(2,1)}, u32[]{:S(2)}) copy-start(bf16[2,4,192,192]{2,3,0,1:T(8,128)(2,1)} %copy.20) | copy-start | bytes 1769476
  72.9 1.4 %copy-start.3 = (bf16[2,4,192,192]{2,3,0,1:T(8,128)(2,1)S(1)}, bf16[2,4,192,192]{2,3,0,1:T(8,128)(2,1)}, u32[]{:S(2)}) copy-start(bf16[2,4,192,192]{2,3,0,1:T(8,128)(2,1)} %copy.21) | copy-start | bytes 1769476

commit v2 on v1

v2 whole, which is shorter than its diff:
```python
import math

import jax
import jax.numpy as jnp
from jax import lax
from jax.experimental import pallas as pl
from jax.experimental.pallas import tpu as pltpu
from jax.sharding import PartitionSpec as P

LX = 32
LY = 32
LZ = 32
NX = 4
NY = 4
NZ = 8
ZLO = 4
NEV = 192
COLS = 2 * NEV
SITES = LX * LY
ROWS = 24
MESH = pl.DeviceIdType.MESH
F32 = jnp.float32
BF16 = jnp.bfloat16


def block_of(z):
    return lax.rem(z, ZLO) * 2 + lax.div(z, ZLO)


def turned(columns):
    lane = lax.broadcasted_iota(jnp.int32, columns.shape, 1)
    return pltpu.roll(columns, NEV, 1) * jnp.where(lane < NEV, 1.0, -1.0)


def exchange(eig, mom, st, peram, src, half, trig, vt, vs, w, dsend, d2d, mine, ysend, yrecv, q, zrecv, eown, xall,
             stall, sel, srecv, sink, pcat,
             p_s, d2d_s, d2d_r, st_s, st_r, y_s, y_r, z_s, z_r, x_s, x_r, sink_s, sink_r, sel_s, sel_r,
             up_s, up_r, out_s, out_r, sib_s, sib_r):
    y = lax.axis_index("src")
    snk = lax.axis_index("snk")
    slab = lax.axis_index("slab")
    zh, x = lax.div(snk, NX), lax.rem(snk, NX)
    zl, c = lax.div(slab, 2), lax.rem(slab, 2)
    z = zh * ZLO + zl
    own = block_of(z)
    picks = x == y

    def at(y=y, x=x, z=None, zh=zh, zl=zl, c=c):
        if z is not None:
            zh, zl = lax.div(z, ZLO), lax.rem(z, ZLO)
        return {"src": y, "snk": zh * NX + x, "slab": zl * 2 + c}

    def turn(value, by, size):
        return lax.rem(value + by, size)

    def copy(source, target, send, recv, device):
        return pltpu.make_async_remote_copy(
            src_ref=source, dst_ref=target, send_sem=send, recv_sem=recv, device_id=device, device_id_type=MESH
        )

    barrier = pltpu.get_barrier_semaphore()
    peers = [at(y=turn(y, k // 4, NY), zh=turn(zh, k // 2 % 2, 2), c=turn(c, k % 2, 2)) for k in range(1, 16)]
    peers += [at(z=turn(z, k, NZ)) for k in (1, 2, 3, 5, 6, 7)]
    peers += [at(x=turn(x, k, NX)) for k in (1, 2, 3)]
    for peer in peers:
        pl.semaphore_signal(barrier, inc=1, device_id=peer, device_id_type=MESH)

    loads = []
    for t in range(2):
        for s in range(2):
            loads.append(pltpu.make_async_copy(peram.at[t, s], pcat.at[t, s, :, pl.ds(0, NEV)], p_s.at[t, s]))
            loads[-1].start()

    sends = []
    sibling = at(c=1 - c)

    row = lax.broadcasted_iota(jnp.int32, (8, SITES), 0)
    site = lax.broadcasted_iota(jnp.int32, (8, SITES), 1)

    def component(k):
        value = jnp.zeros((8, SITES), jnp.int32)
        for d in range(NY):
            value = jnp.where((row & 3) == d, mom[turn(y, d, NY), k], value)
        return value

    plane = y * NZ + slab
    fx = ((component(0) * (site & (LX - 1))) & (LX - 1)).astype(F32) / LX
    fy = ((component(1) * ((site >> 5) & (LY - 1))) & (LY - 1)).astype(F32) / LY
    fz = ((component(2) * plane) & (LZ - 1)).astype(F32) / LZ
    angle = 2.0 * math.pi * (fx + fy + fz)
    trig[...] = jnp.where(row < 4, jnp.cos(angle), jnp.sin(angle)).T

    def prepare(t):
        vt[t] = eig[t].T
        for r in range(0, SITES, 256):
            vs[t, r : r + 256] = turned(eig[t, r : r + 256].astype(F32)).astype(BF16)

    def elemental(t, d, slot):
        for r in range(0, SITES, 128):
            cosine = trig[r : r + 128, d : d + 1]
            sine = trig[r : r + 128, d + 4 : d + 5]
            phased = cosine * eig[t, r : r + 128].astype(F32) + sine * vs[t, r : r + 128].astype(F32)
            w[slot, r : r + 128] = phased.astype(BF16)
        gram = jnp.dot(vt[t], w[slot], preferred_element_type=F32)
        return (gram[:NEV] + turned(gram[NEV:])).reshape(NZ, ROWS, COLS)

    pair = {}

    def give(d):
        dsend[d] = elemental(1 - c, d, d % 2).astype(BF16)
        pair[d] = copy(dsend.at[d], d2d.at[d], d2d_s.at[d], d2d_r.at[d], sibling)

    prepare(1 - c)
    give(1)
    pl.semaphore_wait(barrier, len(peers))
    pair[1].start()
    stall[y] = st[...]
    to_pick = copy(stall.at[y], stall.at[y], st_s, st_r.at[y], at(y=x))
    pl.when(x != y)(to_pick.start)
    for d in (3, 2):
        give(d)
        pair[d].start()

    prepare(c)
    along = []
    for d in (1, 3, 2):
        value = elemental(c, d, d % 2)
        pair[d].wait_recv()
        ysend[d - 1] = (value + d2d[d].astype(F32)).astype(BF16)
        along.append(copy(ysend.at[d - 1], yrecv.at[d - 1], y_s.at[d - 1], y_r.at[d - 1], at(y=turn(y, d, NY))))
        along[-1].start()
    give(0)
    pair[0].start()
    sends += list(pair.values()) + along
    mine[...] = elemental(c, 0, 1)

    for each in loads:
        each.wait()
    at_row = lax.broadcasted_iota(jnp.int32, (COLS, COLS), 0)
    at_col = lax.broadcasted_iota(jnp.int32, (COLS, COLS), 1)
    swap = (jnp.where(at_col == at_row + NEV, 1.0, 0.0) - jnp.where(at_row == at_col + NEV, 1.0, 0.0)).astype(BF16)
    for t in range(2):
        for s in range(2):
            for k in range(4):
                pcat[t, s, k, NEV:] = jnp.dot(pcat[t, s, k, :NEV], swap, preferred_element_type=F32).astype(BF16)

    pair[0].wait_recv()
    for each in along:
        each.wait_recv()

    def summed(block):
        total = mine[block] + d2d[0, block].astype(F32)
        for d in range(3):
            total += yrecv[d, block].astype(F32)
        return total.astype(BF16)

    for dz in (4, 3, 5, 2, 6, 1, 7):
        to = turn(z, dz, NZ)
        q[dz] = summed(block_of(to))
        each = copy(q.at[dz], zrecv.at[z], z_s.at[dz], z_r.at[z], at(z=to))
        each.start()
        sends.append(each)
    zrecv[z] = summed(own)
    for dz in range(1, NZ):
        come = turn(z, dz, NZ)
        copy(q.at[dz], zrecv.at[come], z_s.at[dz], z_r.at[come], at(z=come)).wait_recv()
    for g in range(2):
        total = zrecv[g * ZLO].astype(F32)
        for k in range(1, ZLO):
            total += zrecv[g * ZLO + k].astype(F32)
        eown[g] = total.astype(BF16)

    to_diagonal = copy(eown, xall.at[x], x_s, x_r.at[x], at(x=y))
    pl.when(x != y)(to_diagonal.start)

    def picked(plane, s):
        wanted = stall[plane, s][0:1]
        total = jnp.zeros((ROWS, COLS), F32)
        for k in range(NX):
            for g in range(2):
                total += jnp.where(wanted == 2 * (g * NX + k) + c, xall[k, g].astype(F32), 0.0)
        return total.astype(BF16)

    def pick(dy, ds):
        return copy(sel.at[dy, ds], srecv.at[c], sel_s.at[dy, ds], sel_r.at[c], at(y=turn(y, dy, NY), c=turn(c, ds, 2)))

    moves = ((1, 0), (1, 1), (3, 0), (3, 1), (2, 0), (2, 1), (0, 1))

    @pl.when(picks)
    def _():
        xall[x] = eown[...]
        for d in (1, 2, 3):
            come = turn(x, d, NX)
            copy(eown, xall.at[come], x_s, x_r.at[come], at(x=come)).wait_recv()
            come = turn(y, d, NY)
            copy(stall.at[come], stall.at[come], st_s, st_r.at[come], at(y=come)).wait_recv()
        for dy, ds in moves:
            sel[dy, ds] = picked(turn(y, dy, NY), turn(c, ds, 2))
            pick(dy, ds).start()
        srecv[c] = picked(y, c)

    for dy, dg in ((1, 0), (3, 0), (2, 0), (0, 1), (1, 1), (3, 1), (2, 1)):
        g = turn(zh, dg, 2)
        each = copy(eown.at[g], sink.at[c, y], sink_s.at[dy, dg], sink_r.at[c, y], at(y=turn(y, dy, NY), zh=g, c=zh))
        each.start()
        sends.append(each)
    to_sibling = copy(eown.at[zh], sink.at[c, y], sink_s.at[0, 0], sink_r.at[c, y], sibling)

    @pl.when(c == zh)
    def _():
        sink[c, y] = eown[zh]

    @pl.when(c != zh)
    def _():
        to_sibling.start()

    def come_pick(k):
        copy(sel.at[0, 0], srecv.at[k], sel_s.at[0, 0], sel_r.at[k], at(y=x)).wait_recv()

    come_pick(1 - c)
    pl.when(x != y)(lambda: come_pick(c))
    src[c, x, own] = srecv[0] + srecv[1]

    groups = [(own, 1), (block_of(turn(z, ZLO, NZ)), 1)] + [(turn(zl, k, ZLO) * 2, 2) for k in (1, 2, 3)]

    def piece(s, m, group):
        first, count = groups[group]
        return src.at[s, m, pl.ds(first, count)]

    for dz in (4, 3, 5, 2, 6, 1, 7):
        each = copy(src.at[c, x, own], src.at[c, x, own], up_s.at[dz], up_r.at[z], at(z=turn(z, dz, NZ)))
        each.start()
        sends.append(each)

    def share(group, d):
        m = turn(x, NX - d, NX)
        each = copy(piece(c, m, group), piece(c, m, group), sib_s.at[d, group], sib_r.at[d, group], sibling)
        each.start()
        sends.append(each)

    def spread(group):
        for d in (1, 3, 2):
            each = copy(piece(c, x, group), piece(c, x, group), out_s.at[d - 1, group], out_r.at[d - 1, group],
                        at(x=turn(x, d, NX)))
            each.start()
            sends.append(each)
        share(group, 0)

    spread(0)

    for dy in range(NY):
        for dc in range(2):
            m, k = turn(y, dy, NY), turn(c, dc, 2)
            here = copy(eown.at[0], sink.at[k, m], sink_s.at[dy, dc], sink_r.at[k, m], at(y=m))
            if dy or dc:
                here.wait_recv()
            else:
                pl.when(c != zh)(here.wait_recv)
    for t in range(2):
        left = sink[t].astype(F32).reshape(NY * ROWS, COLS).astype(BF16)
        for s in range(2):
            for k in range(4):
                value = jnp.dot(left, pcat[t, s, k], preferred_element_type=F32)
                value = value.reshape(NY, ROWS, COLS).astype(BF16)
                for m in range(NY):
                    half[s, m, t, k] = value[m]

    def come_up(height):
        copy(src.at[c, x, own], src.at[c, x, block_of(height)], up_s.at[1], up_r.at[height], at(z=height)).wait_recv()

    come_up(turn(z, ZLO, NZ))
    spread(1)
    for k in (1, 3, 2):
        low = turn(zl, k, ZLO)
        come_up(low)
        come_up(low + ZLO)
        spread(1 + k)

    def come_out(group, d):
        m = turn(x, NX - d, NX)
        copy(piece(c, m, group), piece(c, m, group), out_s.at[d - 1, group], out_r.at[d - 1, group], at(x=m)).wait_recv()

    for group in (0, 1, 2, 4, 3):
        for d in (1, 3, 2):
            come_out(group, d)
            share(group, d)
    for group in range(5):
        for d in range(NX):
            m = turn(x, NX - d, NX)
            copy(piece(1 - c, m, group), piece(1 - c, m, group), sib_s.at[d, group], sib_r.at[d, group],
                 sibling).wait_recv()

    for each in sends:
        each.wait_send()
    pl.when(c != zh)(to_sibling.wait_send)

    @pl.when(x != y)
    def _():
        to_pick.wait_send()
        to_diagonal.wait_send()

    @pl.when(picks)
    def _():
        for dy, ds in moves:
            pick(dy, ds).wait_send()


def exchanged(eigvecs, momenta, st, perambulator):
    dma = pltpu.SemaphoreType.DMA

    def vmem(*lead, kind=BF16):
        return pltpu.VMEM(lead + (ROWS, COLS), kind)

    whole = pl.BlockSpec(memory_space=pltpu.VMEM)
    return pl.pallas_call(
        exchange,
        out_shape=(
            jax.ShapeDtypeStruct((2, NY, NZ, ROWS, COLS), BF16),
            jax.ShapeDtypeStruct((2, NY, 2, 4, ROWS, COLS), BF16),
        ),
        in_specs=[whole, pl.BlockSpec(memory_space=pltpu.SMEM), whole, pl.BlockSpec(memory_space=pl.ANY)],
        out_specs=(whole, whole),
        scratch_shapes=[
            pltpu.VMEM((SITES, 8), F32), pltpu.VMEM((2, COLS, SITES), BF16), pltpu.VMEM((2, SITES, COLS), BF16),
            pltpu.VMEM((2, SITES, COLS), BF16),
            vmem(4, 8), vmem(4, 8), vmem(8, kind=F32), vmem(3, 8), vmem(3, 8), vmem(8), vmem(8), vmem(2), vmem(4, 2),
            pltpu.VMEM((4, 2, 8, COLS), jnp.int32), vmem(4, 2), vmem(2), vmem(2, 4),
            pltpu.VMEM((2, 2, 4, COLS, COLS), BF16),
            dma((2, 2)), dma((4,)), dma((4,)), dma, dma((4,)), dma((3,)), dma((3,)), dma((8,)), dma((8,)),
            dma, dma((4,)), dma((4, 2)), dma((2, 4)), dma((4, 2)), dma((2,)),
            dma((8,)), dma((8,)), dma((3, 5)), dma((3, 5)), dma((4, 5)), dma((4, 5)),
        ],
        compiler_params=pltpu.CompilerParams(
            collective_id=0, has_side_effects=True, vmem_limit_bytes=48 * 1024 * 1024
        ),
    )(eigvecs, momenta, st, perambulator)


def product(half, src, out):
    at_row = lax.broadcasted_iota(jnp.int32, (COLS, COLS), 0)
    at_col = lax.broadcasted_iota(jnp.int32, (COLS, COLS), 1)
    swap = (jnp.where(at_col == at_row + NEV, 1.0, 0.0) - jnp.where(at_row == at_col + NEV, 1.0, 0.0)).astype(BF16)
    rows = src[0, 0]
    both = jnp.concatenate([rows, jnp.dot(rows, swap, preferred_element_type=F32).astype(BF16)], axis=0)
    value = lax.dot_general(half[0, 0], both, (((1,), (1,)), ((), ())), preferred_element_type=F32)
    out[0, :, 0] = value.reshape(2, 4, ROWS, COLS)


def local(eigvecs, perambulator, momenta, source_times):
    st = jnp.broadcast_to(source_times[:, None, None], (2, 8, COLS))
    source, half = exchanged(eigvecs, momenta, st, perambulator)
    block = pl.BlockSpec((1, 1, NEV, COLS), lambda m, s: (s, m, 0, 0))
    return pl.pallas_call(
        product,
        grid=(NY, 2),
        out_shape=jax.ShapeDtypeStruct((NY, 2, 2, 4, ROWS, COLS), F32),
        in_specs=[block, block],
        out_specs=pl.BlockSpec((1, 2, 1, 4, ROWS, COLS), lambda m, s: (m, 0, s, 0, 0, 0)),
    )(half.reshape(2, NY, NEV, COLS), source.reshape(2, NY, NEV, COLS))


def solution(mesh):
    placed = (P("snk", ("src", "slab"), None), P("snk", "src", None, None, None), P(), P("src"))
    return jax.shard_map(
        local,
        mesh=mesh,
        in_specs=placed,
        out_specs=P(None, "snk", "src", None, "slab", None),
        check_vma=False,
    )
```

time: 78.4 us -> 66.9 us (0.85)
  other arithmetic: 9.8 us -> 0 us
  Pallas kernels: 52.5 us -> 61.7 us
  matrix products: 6.49 us -> 0 us
  local copies, waits for them, and re-layouts: 9.25 us -> 4.86 us
    pallas_call x1 -> x2, Pallas kernels: 52.5 us -> 61.7 us  [the longest x1 54.2 us: exchanged(): pl.pallas_call(exchange, out_shape=(jax.ShapeDtypeStruct((2, NY, NZ, ROWS...]
    another operation x8 -> x0, other arithmetic: 7.81 us -> none
    dot_general x6 -> x0, matrix products: 6.49 us -> none  [the longest x4 4.68 us: local(): jnp.einsum('tsa,tsb->tab', eigvecs, phased, preferred_element_type=jnp.fl...]
    slice x3 -> x0, local copies, waits for them, and re-layouts: 2.41 us -> none  [the longest x1 1.24 us: local(): both = jnp.concatenate([source[..., :nev], source[..., nev:]], axis=2)]
    concatenate x1 -> x0, local copies, waits for them, and re-layouts: 1.59 us -> none  [local(): return jnp.concatenate([dreal, dimag], axis=-1)]
    concatenate x5 -> x0, other arithmetic: 0.98 us -> none  [the longest x4 0.49 us: local(): partials.append(jnp.concatenate([real, imag], axis=2))]
    add x2 -> x0, other arithmetic: 0.89 us -> none  [the longest x1 0.88 us: local(): dreal = quad[..., :rows, :nev] + quad[..., rows:, nev:]]
    unnamed x10 -> x8, local copies, waits for them, and re-layouts: 4.06 us -> 4.13 us
where the time goes in v2:
time: 66.9 us; the launch traced here: 66.6 us
  Pallas kernels  61.7 us (92%)
  local copies, waits for them, and re-layouts  4.86 us (7%)
    pallas_call x1, Pallas kernels, exchanged(): pl.pallas_call(exchange, out_shape=(jax.ShapeDtypeStruct((2, NY, NZ, ROWS...  54.2 us
    pallas_call x1, Pallas kernels, local(): pl.pallas_call(product, grid=(NY, 2), out_shape=jax.ShapeDtypeStruct((NY,...  7.55 us
    unnamed x8, local copies, waits for them, and re-layouts  4.13 us

profile of v2, /device:TPU:1, one launch (start us, length us, event | category | flops | bytes accessed | tf_op | source)
XLA Modules:
  0.0 66.6 jit_solution(4920330955360804974)
XLA Ops:
  0.0 0.7 %broadcast_in_dim.2.st = s32[2,8,384]{2,1,0:T(8,128)S(1)} broadcast(s32[2]{0:T(128)} %param.7), dimensions={0} | broadcast | bytes 24584 | tf_op jit(solution)/shard_map/broadcast_in_dim | solution.py:350
  0.7 0.0 copy-start
  0.7 1.4 %copy-done = bf16[2,1024,384]{2,1,0:T(8,128)(2,1)S(1)} copy-done((bf16[2,1024,384]{2,1,0:T(8,128)(2,1)S(1)}, bf16[2,1024,384]{2,1,0:T(8,128)(2,1)}, u32[]{:S(2)}) %copy-start) | copy-done | bytes 1572888
  2.1 0.0 copy-start.3
  2.1 0.7 %copy-done.3 = s32[4,3]{1,0:T(4,128)S(1)} copy-done((s32[4,3]{1,0:T(4,128)S(1)}, s32[4,3]{1,0:T(4,128)}, u32[]{:S(2)}) %copy-start.3) | copy-done | bytes 72
  2.8 54.2 %shard_map.46 = (bf16[2,4,8,24,384]{4,3,2,1,0:T(8,128)(2,1)S(1)}, bf16[2,4,2,4,24,384]{5,4,3,2,1,0:T(8,128)(2,1)S(1)}) custom-call(bf16[2,1024,384]{2,1,0:T(8,128)(2,1)S(1)} %copy-done, s32[4,3]{1,0:T(4,128)S(1)} %copy-done.3, s32[2,8,384]{2,1,0:T(8,128)S(1)} %broadcast_in_dim.2.st, bf16[2,2,4,192,384]{4,3,2,1,0:T(8,128)(2,1)} %peram.1), custom_call_target="tpu_custom_call" | custom-call | tf_op jit(solution)/shard_map/pallas_call | solution.py:315
  57.0 0.0 copy-start.1
  57.0 1.0 %copy-done.1 = bf16[2,4,8,24,384]{4,3,2,1,0:T(8,128)(2,1)} copy-done((bf16[2,4,8,24,384]{4,3,2,1,0:T(8,128)(2,1)}, bf16[2,4,8,24,384]{4,3,2,1,0:T(8,128)(2,1)S(1)}, u32[]{:S(2)}) %copy-start.1) | copy-done | bytes 1179672
  58.0 0.0 copy-start.2
  58.0 1.0 %copy-done.2 = bf16[2,4,2,4,24,384]{5,4,3,2,1,0:T(8,128)(2,1)} copy-done((bf16[2,4,2,4,24,384]{5,4,3,2,1,0:T(8,128)(2,1)}, bf16[2,4,2,4,24,384]{5,4,3,2,1,0:T(8,128)(2,1)S(1)}, u32[]{:S(2)}) %copy-start.2) | copy-done | bytes 1179672
  59.0 7.5 %shard_map.47 = f32[4,2,2,4,24,384]{5,4,3,2,1,0:T(8,128)} custom-call(bf16[2,4,192,384]{3,2,1,0:T(8,128)(2,1)} %bitcast.3, bf16[2,4,192,384]{3,2,1,0:T(8,128)(2,1)} %bitcast.2), custom_call_target="tpu_custom_call" | custom-call | tf_op jit(solution)/shard_map/pallas_call | solution.py:353
Async XLA Ops:
  0.7 1.4 %copy-start = (bf16[2,1024,384]{2,1,0:T(8,128)(2,1)S(1)}, bf16[2,1024,384]{2,1,0:T(8,128)(2,1)}, u32[]{:S(2)}) copy-start(bf16[2,1024,384]{2,1,0:T(8,128)(2,1)} %eig.1) | copy-start | bytes 4718596
  2.1 0.7 %copy-start.3 = (s32[4,3]{1,0:T(4,128)S(1)}, s32[4,3]{1,0:T(4,128)}, u32[]{:S(2)}) copy-start(s32[4,3]{1,0:T(4,128)} %mom.1) | copy-start | bytes 148
  57.0 1.0 %copy-start.1 = (bf16[2,4,8,24,384]{4,3,2,1,0:T(8,128)(2,1)}, bf16[2,4,8,24,384]{4,3,2,1,0:T(8,128)(2,1)S(1)}, u32[]{:S(2)}) copy-start(bf16[2,4,8,24,384]{4,3,2,1,0:T(8,128)(2,1)S(1)} %get-tuple-element.8) | copy-start | bytes 3538948
  58.0 1.0 %copy-start.2 = (bf16[2,4,2,4,24,384]{5,4,3,2,1,0:T(8,128)(2,1)}, bf16[2,4,2,4,24,384]{5,4,3,2,1,0:T(8,128)(2,1)S(1)}, u32[]{:S(2)}) copy-start(bf16[2,4,2,4,24,384]{5,4,3,2,1,0:T(8,128)(2,1)S(1)} %get-tuple-element.7) | copy-start | bytes 3538948

commit v3 on v2

v3 whole, which is shorter than its diff:
```python
import math

import jax
import jax.numpy as jnp
from jax import lax
from jax.experimental import pallas as pl
from jax.experimental.pallas import tpu as pltpu
from jax.sharding import PartitionSpec as P

LX = 32
LY = 32
LZ = 32
NX = 4
NY = 4
NZ = 8
ZLO = 4
NEV = 192
COLS = 2 * NEV
SITES = LX * LY
ROWS = 24
MESH = pl.DeviceIdType.MESH
F32 = jnp.float32
BF16 = jnp.bfloat16


def block_of(z):
    return lax.rem(z, ZLO) * 2 + lax.div(z, ZLO)


def turned(columns):
    lane = lax.broadcasted_iota(jnp.int32, columns.shape, 1)
    return pltpu.roll(columns, NEV, 1) * jnp.where(lane < NEV, 1.0, -1.0)


def swap_matrix():
    at_row = lax.broadcasted_iota(jnp.int32, (COLS, COLS), 0)
    at_col = lax.broadcasted_iota(jnp.int32, (COLS, COLS), 1)
    return (jnp.where(at_col == at_row + NEV, 1.0, 0.0) - jnp.where(at_row == at_col + NEV, 1.0, 0.0)).astype(BF16)


def exchange(eigvecs, momenta, source_times, peram, blocks, src, half, both, made, eig, mom, st, trig, vt, vs, w, dsend, d2d, mine, ysend, yrecv, q, zrecv, eown, xall,
             stall, sel, srecv, sink, pcat,
             in_s, p_s, d2d_s, d2d_r, st_s, st_r, y_s, y_r, z_s, z_r, x_s, x_r, sink_s, sink_r, sel_s, sel_r,
             up_s, up_r, out_s, out_r, sib_s, sib_r, made_s):
    y = lax.axis_index("src")
    snk = lax.axis_index("snk")
    slab = lax.axis_index("slab")
    zh, x = lax.div(snk, NX), lax.rem(snk, NX)
    zl, c = lax.div(slab, 2), lax.rem(slab, 2)
    z = zh * ZLO + zl
    own = block_of(z)
    picks = x == y

    def at(y=y, x=x, z=None, zh=zh, zl=zl, c=c):
        if z is not None:
            zh, zl = lax.div(z, ZLO), lax.rem(z, ZLO)
        return {"src": y, "snk": zh * NX + x, "slab": zl * 2 + c}

    def turn(value, by, size):
        return lax.rem(value + by, size)

    def copy(source, target, send, recv, device):
        return pltpu.make_async_remote_copy(
            src_ref=source, dst_ref=target, send_sem=send, recv_sem=recv, device_id=device, device_id_type=MESH
        )

    barrier = pltpu.get_barrier_semaphore()
    peers = [at(y=turn(y, k // 4, NY), zh=turn(zh, k // 2 % 2, 2), c=turn(c, k % 2, 2)) for k in range(1, 16)]
    peers += [at(z=turn(z, k, NZ)) for k in (1, 2, 3, 5, 6, 7)]
    peers += [at(x=turn(x, k, NX)) for k in (1, 2, 3)]
    for peer in peers:
        pl.semaphore_signal(barrier, inc=1, device_id=peer, device_id_type=MESH)

    fetches = [
        pltpu.make_async_copy(momenta, mom, in_s.at[0]),
        pltpu.make_async_copy(source_times, st, in_s.at[1]),
        pltpu.make_async_copy(eigvecs.at[1 - c], eig.at[1 - c], in_s.at[2]),
        pltpu.make_async_copy(eigvecs.at[c], eig.at[c], in_s.at[3]),
    ]
    loads = []
    for t in range(2):
        for s in range(2):
            loads.append(pltpu.make_async_copy(peram.at[t, s], pcat.at[t, s, :, pl.ds(0, NEV)], p_s.at[t, s]))
    for each in fetches + loads:
        each.start()
    fetches[0].wait()

    sends = []
    sibling = at(c=1 - c)

    row = lax.broadcasted_iota(jnp.int32, (8, SITES), 0)
    site = lax.broadcasted_iota(jnp.int32, (8, SITES), 1)

    def component(k):
        value = jnp.zeros((8, SITES), jnp.int32)
        for d in range(NY):
            value = jnp.where((row & 3) == d, mom[turn(y, d, NY), k], value)
        return value

    plane = y * NZ + slab
    fx = ((component(0) * (site & (LX - 1))) & (LX - 1)).astype(F32) / LX
    fy = ((component(1) * ((site >> 5) & (LY - 1))) & (LY - 1)).astype(F32) / LY
    fz = ((component(2) * plane) & (LZ - 1)).astype(F32) / LZ
    angle = 2.0 * math.pi * (fx + fy + fz)
    trig[...] = jnp.where(row < 4, jnp.cos(angle), jnp.sin(angle)).T

    def prepare(t):
        vt[t] = eig[t].T
        for r in range(0, SITES, 256):
            vs[t, r : r + 256] = -jnp.dot(eig[t, r : r + 256], swap, preferred_element_type=F32).astype(BF16)

    def phase(t, d, slot):
        for r in range(0, SITES, 128):
            cosine = trig[r : r + 128, d : d + 1]
            sine = trig[r : r + 128, d + 4 : d + 5]
            phased = cosine * eig[t, r : r + 128].astype(F32) + sine * vs[t, r : r + 128].astype(F32)
            w[slot, r : r + 128] = phased.astype(BF16)

    swap = swap_matrix()
    fetches[2].wait()
    prepare(1 - c)
    fetches[3].wait()
    prepare(c)

    pair = {}
    along = {}
    turns = ((1, 2), (1, 1), (0, 2), (1, 3), (0, 1), (0, 3), (1, 0), (0, 0))

    def time(other):
        return 1 - c if other else c

    def go_along(d):
        pair[d].wait_recv()
        ysend[d - 1] = (mine[d] + d2d[d].astype(F32)).astype(BF16)
        along[d] = copy(ysend.at[d - 1], yrecv.at[d - 1], y_s.at[d - 1], y_r.at[d - 1], at(y=turn(y, d, NY)))
        along[d].start()

    phase(1 - c, 2, 0)
    for k, (other, d) in enumerate(turns):
        if k + 1 < len(turns):
            phase(time(turns[k + 1][0]), turns[k + 1][1], (k + 1) % 2)
        gram = jnp.dot(vt[time(other)], w[k % 2], preferred_element_type=F32)
        value = (gram[:NEV] + turned(gram[NEV:])).reshape(NZ, ROWS, COLS)
        if other:
            dsend[d] = value.astype(BF16)
            pair[d] = copy(dsend.at[d], d2d.at[d], d2d_s.at[d], d2d_r.at[d], sibling)
        else:
            mine[d] = value
        if k == 3:
            pl.semaphore_wait(barrier, len(peers))
            for each in (2, 1, 3):
                pair[each].start()
            fetches[1].wait()
            for s in range(2):
                stall[y, s] = jnp.full((8, COLS), st[s], jnp.int32)
            to_pick = copy(stall.at[y], stall.at[y], st_s, st_r.at[y], at(y=x))
            pl.when(x != y)(to_pick.start)
        if k == 4:
            go_along(2)
            go_along(1)
        if k == 5:
            go_along(3)
        if k == 6:
            pair[0].start()
    along = [along[d] for d in (2, 1, 3)]
    sends += list(pair.values()) + along

    for each in loads:
        each.wait()
    for t in range(2):
        for s in range(2):
            for k in range(4):
                pcat[t, s, k, NEV:] = jnp.dot(pcat[t, s, k, :NEV], swap, preferred_element_type=F32).astype(BF16)

    pair[0].wait_recv()
    for each in along:
        each.wait_recv()

    def summed(block):
        total = mine[0, block] + d2d[0, block].astype(F32)
        for d in range(3):
            total += yrecv[d, block].astype(F32)
        return total.astype(BF16)

    for dz in (4, 3, 5, 2, 6, 1, 7):
        to = turn(z, dz, NZ)
        q[dz] = summed(block_of(to))
        each = copy(q.at[dz], zrecv.at[z], z_s.at[dz], z_r.at[z], at(z=to))
        each.start()
        sends.append(each)
    zrecv[z] = summed(own)
    for dz in range(1, NZ):
        come = turn(z, dz, NZ)
        copy(q.at[dz], zrecv.at[come], z_s.at[dz], z_r.at[come], at(z=come)).wait_recv()
    for g in range(2):
        total = zrecv[g * ZLO].astype(F32)
        for k in range(1, ZLO):
            total += zrecv[g * ZLO + k].astype(F32)
        eown[g] = total.astype(BF16)

    to_diagonal = copy(eown, xall.at[x], x_s, x_r.at[x], at(x=y))
    pl.when(x != y)(to_diagonal.start)

    for dy, dg in ((1, 0), (3, 0), (2, 0), (0, 1), (1, 1), (3, 1), (2, 1)):
        g = turn(zh, dg, 2)
        each = copy(eown.at[g], sink.at[c, y], sink_s.at[dy, dg], sink_r.at[c, y], at(y=turn(y, dy, NY), zh=g, c=zh))
        each.start()
        sends.append(each)
    to_sibling = copy(eown.at[zh], sink.at[c, y], sink_s.at[0, 0], sink_r.at[c, y], sibling)

    @pl.when(c == zh)
    def _():
        sink[c, y] = eown[zh]

    @pl.when(c != zh)
    def _():
        to_sibling.start()

    def picked(plane, s):
        wanted = stall[plane, s][0:1]
        total = jnp.zeros((ROWS, COLS), F32)
        for k in range(NX):
            for g in range(2):
                total += jnp.where(wanted == 2 * (g * NX + k) + c, xall[k, g].astype(F32), 0.0)
        return total.astype(BF16)

    def pick(dy, ds):
        return copy(sel.at[dy, ds], srecv.at[c], sel_s.at[dy, ds], sel_r.at[c], at(y=turn(y, dy, NY), c=turn(c, ds, 2)))

    moves = ((1, 0), (1, 1), (3, 0), (3, 1), (2, 0), (2, 1), (0, 1))

    @pl.when(picks)
    def _():
        xall[x] = eown[...]
        for d in (1, 2, 3):
            come = turn(x, d, NX)
            copy(eown, xall.at[come], x_s, x_r.at[come], at(x=come)).wait_recv()
            come = turn(y, d, NY)
            copy(stall.at[come], stall.at[come], st_s, st_r.at[come], at(y=come)).wait_recv()
        for dy, ds in moves:
            sel[dy, ds] = picked(turn(y, dy, NY), turn(c, ds, 2))
            pick(dy, ds).start()
        srecv[c] = picked(y, c)

    def come_pick(k):
        copy(sel.at[0, 0], srecv.at[k], sel_s.at[0, 0], sel_r.at[k], at(y=x)).wait_recv()

    come_pick(1 - c)
    pl.when(x != y)(lambda: come_pick(c))
    src[c, x, own] = srecv[0] + srecv[1]

    order = (0, 1, 7, 2, 6, 3, 5, 4)

    def piece(s, m, group):
        return src.at[s, m, block_of(turn(z, order[group], NZ))]

    for dz in (4, 3, 5, 2, 6, 1, 7):
        each = copy(src.at[c, x, own], src.at[c, x, own], up_s.at[dz], up_r.at[z], at(z=turn(z, dz, NZ)))
        each.start()
        sends.append(each)

    def share(group, d):
        m = turn(x, NX - d, NX)
        each = copy(piece(c, m, group), piece(c, m, group), sib_s.at[d, group], sib_r.at[d, group], sibling)
        each.start()
        sends.append(each)

    def spread(group):
        for d in (1, 3, 2):
            each = copy(piece(c, x, group), piece(c, x, group), out_s.at[d - 1, group], out_r.at[d - 1, group],
                        at(x=turn(x, d, NX)))
            each.start()
            sends.append(each)
        share(group, 0)

    spread(0)

    for dy in range(NY):
        for dc in range(2):
            m, k = turn(y, dy, NY), turn(c, dc, 2)
            here = copy(eown.at[0], sink.at[k, m], sink_s.at[dy, dc], sink_r.at[k, m], at(y=m))
            if dy or dc:
                here.wait_recv()
            else:
                pl.when(c != zh)(here.wait_recv)
    for t in range(2):
        left = sink[t].astype(F32).reshape(NY * ROWS, COLS).astype(BF16)
        for s in range(2):
            for k in range(4):
                value = jnp.dot(left, pcat[t, s, k], preferred_element_type=F32)
                value = value.reshape(NY, ROWS, COLS).astype(BF16)
                for m in range(NY):
                    half[s, m, 4 * t + k] = value[m]

    def come_up(height):
        copy(src.at[c, x, own], src.at[c, x, block_of(height)], up_s.at[1], up_r.at[height], at(z=height)).wait_recv()

    for group in range(1, NZ):
        come_up(turn(z, order[group], NZ))
        spread(group)

    def come_out(group, d):
        m = turn(x, NX - d, NX)
        copy(piece(c, m, group), piece(c, m, group), out_s.at[d - 1, group], out_r.at[d - 1, group], at(x=m)).wait_recv()

    def come_shared(group, d):
        m = turn(x, NX - d, NX)
        copy(piece(1 - c, m, group), piece(1 - c, m, group), sib_s.at[d, group], sib_r.at[d, group], sibling).wait_recv()

    written = []

    def flat(value):
        return value.astype(F32).reshape(NEV, COLS).astype(BF16)

    def finish(s, d):
        slot, m = len(written), turn(x, NX - d, NX)
        rows = flat(src[s, m])
        both[slot % 2, :NEV] = rows
        both[slot % 2, NEV:] = jnp.dot(rows, swap, preferred_element_type=F32).astype(BF16)
        value = lax.dot_general(
            flat(half[s, m]), both[slot % 2], (((1,), (1,)), ((), ())), preferred_element_type=F32
        )
        made[slot] = value.reshape(2, 4, ROWS, COLS)
        written.append(pltpu.make_async_copy(made.at[slot], blocks.at[m, :, s], made_s.at[slot]))
        written[-1].start()

    early = 3
    for group in range(early):
        for d in (1, 3, 2):
            come_out(group, d)
            share(group, d)
    finish(c, 0)
    for group in range(NZ):
        come_shared(group, 0)
    finish(1 - c, 0)
    for group in range(early, NZ):
        for d in (1, 3, 2):
            come_out(group, d)
            share(group, d)
    for d in (1, 3, 2):
        finish(c, d)
    for d in (1, 3, 2):
        for group in range(NZ):
            come_shared(group, d)
        finish(1 - c, d)

    for each in written:
        each.wait()
    for each in sends:
        each.wait_send()
    pl.when(c != zh)(to_sibling.wait_send)

    @pl.when(x != y)
    def _():
        to_pick.wait_send()
        to_diagonal.wait_send()

    @pl.when(picks)
    def _():
        for dy, ds in moves:
            pick(dy, ds).wait_send()


def exchanged(eigvecs, momenta, source_times, perambulator):
    dma = pltpu.SemaphoreType.DMA

    def vmem(*lead, kind=BF16):
        return pltpu.VMEM(lead + (ROWS, COLS), kind)

    return pl.pallas_call(
        exchange,
        out_shape=jax.ShapeDtypeStruct((NY, 2, 2, 4, ROWS, COLS), F32),
        in_specs=[pl.BlockSpec(memory_space=pltpu.HBM)] * 4,
        out_specs=pl.BlockSpec(memory_space=pltpu.HBM),
        scratch_shapes=[
            vmem(2, 4, 8), vmem(2, 4, 8), pltpu.VMEM((2, COLS, COLS), BF16), vmem(8, 2, 4, kind=F32),
            pltpu.VMEM((2, SITES, COLS), BF16), pltpu.SMEM((NY, 3), jnp.int32), pltpu.SMEM((2,), jnp.int32),
            pltpu.VMEM((SITES, 8), F32), pltpu.VMEM((2, COLS, SITES), BF16), pltpu.VMEM((2, SITES, COLS), BF16),
            pltpu.VMEM((2, SITES, COLS), BF16),
            vmem(4, 8), vmem(4, 8), vmem(4, 8, kind=F32), vmem(3, 8), vmem(3, 8), vmem(8), vmem(8), vmem(2), vmem(4, 2),
            pltpu.VMEM((4, 2, 8, COLS), jnp.int32), vmem(4, 2), vmem(2), vmem(2, 4),
            pltpu.VMEM((2, 2, 4, COLS, COLS), BF16),
            dma((4,)), dma((2, 2)), dma((4,)), dma((4,)), dma, dma((4,)), dma((3,)), dma((3,)), dma((8,)), dma((8,)),
            dma, dma((4,)), dma((4, 2)), dma((2, 4)), dma((4, 2)), dma((2,)),
            dma((8,)), dma((8,)), dma((3, 8)), dma((3, 8)), dma((4, 8)), dma((4, 8)), dma((8,)),
        ],
        compiler_params=pltpu.CompilerParams(
            collective_id=0, has_side_effects=True, vmem_limit_bytes=58 * 1024 * 1024
        ),
    )(eigvecs, momenta, source_times, perambulator)


def local(eigvecs, perambulator, momenta, source_times):
    return exchanged(eigvecs, momenta, source_times, perambulator)


def solution(mesh):
    placed = (P("snk", ("src", "slab"), None), P("snk", "src", None, None, None), P(), P("src"))
    return jax.shard_map(
        local,
        mesh=mesh,
        in_specs=placed,
        out_specs=P(None, "snk", "src", None, "slab", None),
        check_vma=False,
    )
```

time: 66.9 us -> 57 us (0.85)
  Pallas kernels: 61.7 us -> 53.6 us
  local copies, waits for them, and re-layouts: 4.86 us -> 3.24 us
    pallas_call x2 -> x1, Pallas kernels: 61.7 us -> 53.6 us  [exchanged(): pl.pallas_call(exchange, out_shape=jax.ShapeDtypeStruct((NY, 2, 2, 4, ROW...]
    unnamed x8 -> x1, local copies, waits for them, and re-layouts: 4.13 us -> 3.24 us
    broadcast_in_dim x1 -> x0, local copies, waits for them, and re-layouts: 0.72 us -> none  [local(): st = jnp.broadcast_to(source_times[:, None, None], (2, 8, COLS))]
where the time goes in v3:
time: 57 us; the launch traced here: 56.9 us
  Pallas kernels  53.6 us (94%)
  local copies, waits for them, and re-layouts  3.24 us (6%)
    pallas_call x1, Pallas kernels, exchanged(): pl.pallas_call(exchange, out_shape=jax.ShapeDtypeStruct((NY, 2, 2, 4, ROW...  53.6 us
    unnamed x1, local copies, waits for them, and re-layouts  3.24 us

profile of v3, /device:TPU:1, one launch (start us, length us, event | category | flops | bytes accessed | tf_op | source)
XLA Modules:
  0.0 56.9 jit_solution(12264484573599700757)
XLA Ops:
  0.0 53.6 %shard_map.46 = f32[4,2,2,4,24,384]{5,4,3,2,1,0:T(8,128)} custom-call(bf16[2,1024,384]{2,1,0:T(8,128)(2,1)} %eigvecs.1, s32[4,3]{1,0:T(4,128)} %momenta.1, s32[2]{0:T(128)} %source_times.1, bf16[2,2,4,192,384]{4,3,2,1,0:T(8,128)(2,1)} %peram.1), custom_call_target="tpu_custom_call" | custom-call | tf_op jit(solution)/shard_map/pallas_call | solution.py:370
  53.6 3.2 %copy.6 = f32[4,2,2,4,24,384]{5,4,3,2,1,0:T(8,128)} copy(f32[4,2,2,4,24,384]{5,4,3,2,1,0:T(8,128)} %shard_map.46) | data formatting | bytes 4718592

commit v4 on v3

--- a/solution.py
+++ b/solution.py
@@ -38,10 +38,10 @@
     return (jnp.where(at_col == at_row + NEV, 1.0, 0.0) - jnp.where(at_row == at_col + NEV, 1.0, 0.0)).astype(BF16)
 
 
-def exchange(eigvecs, momenta, source_times, peram, blocks, src, half, both, made, eig, mom, st, trig, vt, vs, w, dsend, d2d, mine, ysend, yrecv, q, zrecv, eown, xall,
+def exchange(eigvecs, momenta, source_times, peram, blocks, src, half, both, eig, mom, st, trig, vt, vs, w, dsend, d2d, mine, ysend, yrecv, q, zrecv, eown, xall,
              stall, sel, srecv, sink, pcat,
              in_s, p_s, d2d_s, d2d_r, st_s, st_r, y_s, y_r, z_s, z_r, x_s, x_r, sink_s, sink_r, sel_s, sel_r,
-             up_s, up_r, out_s, out_r, sib_s, sib_r, made_s):
+             up_s, up_r, out_s, out_r, sib_s, sib_r):
     y = lax.axis_index("src")
     snk = lax.axis_index("snk")
     slab = lax.axis_index("slab")
@@ -81,7 +81,7 @@
     for t in range(2):
         for s in range(2):
             loads.append(pltpu.make_async_copy(peram.at[t, s], pcat.at[t, s, :, pl.ds(0, NEV)], p_s.at[t, s]))
-    for each in fetches + loads:
+    for each in fetches:
         each.start()
     fetches[0].wait()
 
@@ -101,8 +101,8 @@
     fx = ((component(0) * (site & (LX - 1))) & (LX - 1)).astype(F32) / LX
     fy = ((component(1) * ((site >> 5) & (LY - 1))) & (LY - 1)).astype(F32) / LY
     fz = ((component(2) * plane) & (LZ - 1)).astype(F32) / LZ
-    angle = 2.0 * math.pi * (fx + fy + fz)
-    trig[...] = jnp.where(row < 4, jnp.cos(angle), jnp.sin(angle)).T
+    angle = 2.0 * math.pi * (fx + fy + fz - jnp.where(row < 4, 0.0, 0.25))
+    trig[...] = jnp.cos(angle).T
 
     def prepare(t):
         vt[t] = eig[t].T
@@ -119,8 +119,6 @@
     swap = swap_matrix()
     fetches[2].wait()
     prepare(1 - c)
-    fetches[3].wait()
-    prepare(c)
 
     pair = {}
     along = {}
@@ -137,6 +135,11 @@
 
     phase(1 - c, 2, 0)
     for k, (other, d) in enumerate(turns):
+        if k == 1:
+            fetches[3].wait()
+            for each in loads:
+                each.start()
+            prepare(c)
         if k + 1 < len(turns):
             phase(time(turns[k + 1][0]), turns[k + 1][1], (k + 1) % 2)
         gram = jnp.dot(vt[time(other)], w[k % 2], preferred_element_type=F32)
@@ -146,22 +149,19 @@
             pair[d] = copy(dsend.at[d], d2d.at[d], d2d_s.at[d], d2d_r.at[d], sibling)
         else:
             mine[d] = value
-        if k == 3:
+        if k == 1:
             pl.semaphore_wait(barrier, len(peers))
-            for each in (2, 1, 3):
+            for each in (2, 1):
                 pair[each].start()
             fetches[1].wait()
             for s in range(2):
                 stall[y, s] = jnp.full((8, COLS), st[s], jnp.int32)
             to_pick = copy(stall.at[y], stall.at[y], st_s, st_r.at[y], at(y=x))
             pl.when(x != y)(to_pick.start)
-        if k == 4:
-            go_along(2)
-            go_along(1)
-        if k == 5:
-            go_along(3)
-        if k == 6:
-            pair[0].start()
+        elif k and other:
+            pair[d].start()
+        elif k and d:
+            go_along(d)
     along = [along[d] for d in (2, 1, 3)]
     sends += list(pair.values()) + along
 
@@ -274,6 +274,13 @@
         share(group, 0)
 
     spread(0)
+
+    def come_up(height):
+        copy(src.at[c, x, own], src.at[c, x, block_of(height)], up_s.at[1], up_r.at[height], at(z=height)).wait_recv()
+
+    for group in range(1, NZ):
+        come_up(turn(z, order[group], NZ))
+        spread(group)
 
     for dy in range(NY):
         for dc in range(2):
@@ -292,13 +299,6 @@
                 for m in range(NY):
                     half[s, m, 4 * t + k] = value[m]
 
-    def come_up(height):
-        copy(src.at[c, x, own], src.at[c, x, block_of(height)], up_s.at[1], up_r.at[height], at(z=height)).wait_recv()
-
-    for group in range(1, NZ):
-        come_up(turn(z, order[group], NZ))
-        spread(group)
-
     def come_out(group, d):
         m = turn(x, NX - d, NX)
         copy(piece(c, m, group), piece(c, m, group), out_s.at[d - 1, group], out_r.at[d - 1, group], at(x=m)).wait_recv()
@@ -307,22 +307,21 @@
         m = turn(x, NX - d, NX)
         copy(piece(1 - c, m, group), piece(1 - c, m, group), sib_s.at[d, group], sib_r.at[d, group], sibling).wait_recv()
 
-    written = []
 
     def flat(value):
         return value.astype(F32).reshape(NEV, COLS).astype(BF16)
 
     def finish(s, d):
-        slot, m = len(written), turn(x, NX - d, NX)
+        slot, m = d, turn(x, NX - d, NX)
         rows = flat(src[s, m])
         both[slot % 2, :NEV] = rows
         both[slot % 2, NEV:] = jnp.dot(rows, swap, preferred_element_type=F32).astype(BF16)
         value = lax.dot_general(
             flat(half[s, m]), both[slot % 2], (((1,), (1,)), ((), ())), preferred_element_type=F32
         )
-        made[slot] = value.reshape(2, 4, ROWS, COLS)
-        written.append(pltpu.make_async_copy(made.at[slot], blocks.at[m, :, s], made_s.at[slot]))
-        written[-1].start()
+        value = value.reshape(2, 4, ROWS, COLS)
+        for t in range(2):
+            blocks[m, t, s] = value[t]
 
     early = 3
     for group in range(early):
@@ -344,8 +343,6 @@
             come_shared(group, d)
         finish(1 - c, d)
 
-    for each in written:
-        each.wait()
     for each in sends:
         each.wait_send()
     pl.when(c != zh)(to_sibling.wait_send)
@@ -371,9 +368,9 @@
         exchange,
         out_shape=jax.ShapeDtypeStruct((NY, 2, 2, 4, ROWS, COLS), F32),
         in_specs=[pl.BlockSpec(memory_space=pltpu.HBM)] * 4,
-        out_specs=pl.BlockSpec(memory_space=pltpu.HBM),
+        out_specs=pl.BlockSpec(memory_space=pltpu.VMEM),
         scratch_shapes=[
-            vmem(2, 4, 8), vmem(2, 4, 8), pltpu.VMEM((2, COLS, COLS), BF16), vmem(8, 2, 4, kind=F32),
+            vmem(2, 4, 8), vmem(2, 4, 8), pltpu.VMEM((2, COLS, COLS), BF16),
             pltpu.VMEM((2, SITES, COLS), BF16), pltpu.SMEM((NY, 3), jnp.int32), pltpu.SMEM((2,), jnp.int32),
             pltpu.VMEM((SITES, 8), F32), pltpu.VMEM((2, COLS, SITES), BF16), pltpu.VMEM((2, SITES, COLS), BF16),
             pltpu.VMEM((2, SITES, COLS), BF16),
@@ -382,16 +379,19 @@
             pltpu.VMEM((2, 2, 4, COLS, COLS), BF16),
             dma((4,)), dma((2, 2)), dma((4,)), dma((4,)), dma, dma((4,)), dma((3,)), dma((3,)), dma((8,)), dma((8,)),
             dma, dma((4,)), dma((4, 2)), dma((2, 4)), dma((4, 2)), dma((2,)),
-            dma((8,)), dma((8,)), dma((3, 8)), dma((3, 8)), dma((4, 8)), dma((4, 8)), dma((8,)),
+            dma((8,)), dma((8,)), dma((3, 8)), dma((3, 8)), dma((4, 8)), dma((4, 8)),
         ],
         compiler_params=pltpu.CompilerParams(
-            collective_id=0, has_side_effects=True, vmem_limit_bytes=58 * 1024 * 1024
+            collective_id=0, has_side_effects=True, vmem_limit_bytes=50 * 1024 * 1024
         ),
     )(eigvecs, momenta, source_times, perambulator)
 
 
 def local(eigvecs, perambulator, momenta, source_times):
-    return exchanged(eigvecs, momenta, source_times, perambulator)
+    def here(value):
+        return pltpu.with_memory_space_constraint(value, pltpu.HBM)
+
+    return exchanged(here(eigvecs), here(momenta), here(source_times), here(perambulator))
 
 
 def solution(mesh):

time: 57 us -> 53.9 us (0.946)
  local copies, waits for them, and re-layouts: 3.24 us -> 1.41 us
  Pallas kernels: 53.6 us -> 52.4 us
    unnamed x1, local copies, waits for them, and re-layouts: 3.24 us -> 1.41 us
    pallas_call x1, Pallas kernels: 53.6 us -> 52.4 us  [exchanged(): pl.pallas_call(exchange, out_shape=jax.ShapeDtypeStruct((NY, 2, 2, 4, ROW...]
where the time goes in v4:
time: 53.9 us; the launch traced here: 53.8 us
  Pallas kernels  52.4 us (97%)
  local copies, waits for them, and re-layouts  1.41 us (3%)
    pallas_call x1, Pallas kernels, exchanged(): pl.pallas_call(exchange, out_shape=jax.ShapeDtypeStruct((NY, 2, 2, 4, ROW...  52.4 us
    unnamed x1, local copies, waits for them, and re-layouts  1.41 us

profile of v4, /device:TPU:1, one launch (start us, length us, event | category | flops | bytes accessed | tf_op | source)
XLA Modules:
  0.0 53.8 jit_solution(377821654369930355)
XLA Ops:
  0.0 52.4 %shard_map.46 = f32[4,2,2,4,24,384]{5,4,3,2,1,0:T(8,128)S(1)} custom-call(bf16[2,1024,384]{2,1,0:T(8,128)(2,1)} %eigvecs.1, s32[4,3]{1,0:T(4,128)} %momenta.1, s32[2]{0:T(128)} %source_times.1, bf16[2,2,4,192,384]{4,3,2,1,0:T(8,128)(2,1)} %peram.1), custom_call_target="tpu_custom_call" | custom-call | tf_op jit(solution)/shard_map/pallas_call | solution.py:367
  52.4 1.4 %copy.6 = f32[4,2,2,4,24,384]{5,4,3,2,1,0:T(8,128)} copy(f32[4,2,2,4,24,384]{5,4,3,2,1,0:T(8,128)S(1)} %shard_map.46) | data formatting | bytes 4718592

commit v5 on v4

--- a/solution.py
+++ b/solution.py
@@ -38,10 +38,10 @@
     return (jnp.where(at_col == at_row + NEV, 1.0, 0.0) - jnp.where(at_row == at_col + NEV, 1.0, 0.0)).astype(BF16)
 
 
-def exchange(eigvecs, momenta, source_times, peram, blocks, src, half, both, eig, mom, st, trig, vt, vs, w, dsend, d2d, mine, ysend, yrecv, q, zrecv, eown, xall,
-             stall, sel, srecv, sink, pcat,
-             in_s, p_s, d2d_s, d2d_r, st_s, st_r, y_s, y_r, z_s, z_r, x_s, x_r, sink_s, sink_r, sel_s, sel_r,
-             up_s, up_r, out_s, out_r, sib_s, sib_r):
+def exchange(eigvecs, momenta, source_times, peram, blocks, src, half, both, eig, mom, st, trig, vt, vs, w, dsend, d2d,
+             mine, ysend, yrecv, q, zrecv, xall, stall, sel, es, ep, sink, pcat,
+             in_s, p_s, d2d_s, d2d_r, st_s, st_r, y_s, y_r, z_s, z_r, x_s, x_r, sel_s, sel_r,
+             es_s, es_r, ep_s, ep_r, sink_s, sink_r, up_s, up_r, out_s, out_r, sib_s, sib_r):
     y = lax.axis_index("src")
     snk = lax.axis_index("snk")
     slab = lax.axis_index("slab")
@@ -63,13 +63,6 @@
         return pltpu.make_async_remote_copy(
             src_ref=source, dst_ref=target, send_sem=send, recv_sem=recv, device_id=device, device_id_type=MESH
         )
-
-    barrier = pltpu.get_barrier_semaphore()
-    peers = [at(y=turn(y, k // 4, NY), zh=turn(zh, k // 2 % 2, 2), c=turn(c, k % 2, 2)) for k in range(1, 16)]
-    peers += [at(z=turn(z, k, NZ)) for k in (1, 2, 3, 5, 6, 7)]
-    peers += [at(x=turn(x, k, NX)) for k in (1, 2, 3)]
-    for peer in peers:
-        pl.semaphore_signal(barrier, inc=1, device_id=peer, device_id_type=MESH)
 
     fetches = [
         pltpu.make_async_copy(momenta, mom, in_s.at[0]),
@@ -83,7 +76,16 @@
             loads.append(pltpu.make_async_copy(peram.at[t, s], pcat.at[t, s, :, pl.ds(0, NEV)], p_s.at[t, s]))
     for each in fetches:
         each.start()
+
+    barrier = pltpu.get_barrier_semaphore()
+    peers = [at(z=turn(z, k, NZ)) for k in (4, 3, 5)] + [at(x=turn(x, 2, NX), c=k) for k in range(2)]
+    peers += [at(y=turn(y, 2, NY))] + [at(z=turn(z, k, NZ)) for k in (2, 6)]
+    peers += [at(x=turn(x, d, NX), c=k) for d in (1, 3) for k in range(2)]
+    peers += [at(y=turn(y, d, NY)) for d in (1, 3)] + [at(z=turn(z, k, NZ)) for k in (1, 7)] + [at(c=1 - c)]
+    for peer in peers:
+        pl.semaphore_signal(barrier, inc=1, device_id=peer, device_id_type=MESH)
     fetches[0].wait()
+    fetches[2].wait()
 
     sends = []
     sibling = at(c=1 - c)
@@ -117,7 +119,6 @@
             w[slot, r : r + 128] = phased.astype(BF16)
 
     swap = swap_matrix()
-    fetches[2].wait()
     prepare(1 - c)
 
     pair = {}
@@ -196,66 +197,61 @@
         total = zrecv[g * ZLO].astype(F32)
         for k in range(1, ZLO):
             total += zrecv[g * ZLO + k].astype(F32)
-        eown[g] = total.astype(BF16)
-
-    to_diagonal = copy(eown, xall.at[x], x_s, x_r.at[x], at(x=y))
-    pl.when(x != y)(to_diagonal.start)
-
-    for dy, dg in ((1, 0), (3, 0), (2, 0), (0, 1), (1, 1), (3, 1), (2, 1)):
-        g = turn(zh, dg, 2)
-        each = copy(eown.at[g], sink.at[c, y], sink_s.at[dy, dg], sink_r.at[c, y], at(y=turn(y, dy, NY), zh=g, c=zh))
+        es[y, g] = total.astype(BF16)
+
+    def to_diagonal(k):
+        return copy(es.at[y], xall.at[x, c], x_s.at[k], x_r.at[x, c], at(x=y, c=turn(c, k, 2)))
+
+    @pl.when(x != y)
+    def _():
+        for k in range(2):
+            to_diagonal(k).start()
+
+    for d in (2, 1, 3):
+        each = copy(es.at[y], es.at[y], es_s.at[d - 1], es_r.at[y], at(y=turn(y, d, NY)))
         each.start()
         sends.append(each)
-    to_sibling = copy(eown.at[zh], sink.at[c, y], sink_s.at[0, 0], sink_r.at[c, y], sibling)
-
-    @pl.when(c == zh)
-    def _():
-        sink[c, y] = eown[zh]
-
-    @pl.when(c != zh)
-    def _():
-        to_sibling.start()
-
-    def picked(plane, s):
-        wanted = stall[plane, s][0:1]
+
+    def picked(plane):
+        wanted = stall[plane, c][0:1]
         total = jnp.zeros((ROWS, COLS), F32)
         for k in range(NX):
-            for g in range(2):
-                total += jnp.where(wanted == 2 * (g * NX + k) + c, xall[k, g].astype(F32), 0.0)
+            for parity in range(2):
+                for g in range(2):
+                    total += jnp.where(wanted == 2 * (g * NX + k) + parity, xall[k, parity, g].astype(F32), 0.0)
         return total.astype(BF16)
 
-    def pick(dy, ds):
-        return copy(sel.at[dy, ds], srecv.at[c], sel_s.at[dy, ds], sel_r.at[c], at(y=turn(y, dy, NY), c=turn(c, ds, 2)))
-
-    moves = ((1, 0), (1, 1), (3, 0), (3, 1), (2, 0), (2, 1), (0, 1))
+    def pick(dy):
+        return copy(sel.at[dy], src.at[c, x, 0], sel_s.at[dy], sel_r, at(y=turn(y, dy, NY)))
 
     @pl.when(picks)
     def _():
-        xall[x] = eown[...]
-        for d in (1, 2, 3):
-            come = turn(x, d, NX)
-            copy(eown, xall.at[come], x_s, x_r.at[come], at(x=come)).wait_recv()
-            come = turn(y, d, NY)
-            copy(stall.at[come], stall.at[come], st_s, st_r.at[come], at(y=come)).wait_recv()
-        for dy, ds in moves:
-            sel[dy, ds] = picked(turn(y, dy, NY), turn(c, ds, 2))
-            pick(dy, ds).start()
-        srecv[c] = picked(y, c)
-
-    def come_pick(k):
-        copy(sel.at[0, 0], srecv.at[k], sel_s.at[0, 0], sel_r.at[k], at(y=x)).wait_recv()
-
-    come_pick(1 - c)
-    pl.when(x != y)(lambda: come_pick(c))
-    src[c, x, own] = srecv[0] + srecv[1]
-
-    order = (0, 1, 7, 2, 6, 3, 5, 4)
+        to_diagonal(1).start()
+        xall[x, c] = es[y]
+        for d in (0, 1, 3, 2):
+            for k in range(2):
+                if d or k:
+                    come, parity = turn(x, d, NX), turn(c, k, 2)
+                    copy(es.at[y], xall.at[come, parity], x_s.at[k], x_r.at[come, parity], at(x=come, c=1 - c)).wait_recv()
+            if d:
+                come = turn(y, d, NY)
+                copy(stall.at[come], stall.at[come], st_s, st_r.at[come], at(y=come)).wait_recv()
+        for dy in (2, 1, 3):
+            sel[dy] = picked(turn(y, dy, NY))
+            pick(dy).start()
+        src[c, x, 0] = picked(y)
+
+    @pl.when(x != y)
+    def _():
+        pick(1).wait_recv()
+
+    groups = ((0, 1), (1, 2), (6, 2), (3, 3))
 
     def piece(s, m, group):
-        return src.at[s, m, block_of(turn(z, order[group], NZ))]
-
-    for dz in (4, 3, 5, 2, 6, 1, 7):
-        each = copy(src.at[c, x, own], src.at[c, x, own], up_s.at[dz], up_r.at[z], at(z=turn(z, dz, NZ)))
+        return src.at[s, m, pl.ds(groups[group][0], groups[group][1])]
+
+    for dz in (1, 7, 2, 6, 3, 5, 4):
+        each = copy(src.at[c, x, 0], src.at[c, x, NZ - dz], up_s.at[dz], up_r.at[NZ - dz], at(z=turn(z, dz, NZ)))
         each.start()
         sends.append(each)
 
@@ -266,7 +262,7 @@
         sends.append(each)
 
     def spread(group):
-        for d in (1, 3, 2):
+        for d in (2, 1, 3):
             each = copy(piece(c, x, group), piece(c, x, group), out_s.at[d - 1, group], out_r.at[d - 1, group],
                         at(x=turn(x, d, NX)))
             each.start()
@@ -275,21 +271,53 @@
 
     spread(0)
 
-    def come_up(height):
-        copy(src.at[c, x, own], src.at[c, x, block_of(height)], up_s.at[1], up_r.at[height], at(z=height)).wait_recv()
-
-    for group in range(1, NZ):
-        come_up(turn(z, order[group], NZ))
+    for d in (1, 2, 3):
+        m = turn(y, d, NY)
+        copy(es.at[m], es.at[m], es_s.at[d - 1], es_r.at[m], at(y=m)).wait_recv()
+    opposite = copy(es.at[:, 1 - zh], ep, ep_s, ep_r, at(z=turn(z, ZLO, NZ)))
+    opposite.start()
+    sends.append(opposite)
+
+    for group in (1, 2, 3):
+        for k in range(groups[group][0], sum(groups[group])):
+            copy(src.at[c, x, 0], src.at[c, x, k], up_s.at[1], up_r.at[k], at(z=turn(z, k, NZ))).wait_recv()
         spread(group)
 
-    for dy in range(NY):
-        for dc in range(2):
-            m, k = turn(y, dy, NY), turn(c, dc, 2)
-            here = copy(eown.at[0], sink.at[k, m], sink_s.at[dy, dc], sink_r.at[k, m], at(y=m))
-            if dy or dc:
-                here.wait_recv()
-            else:
-                pl.when(c != zh)(here.wait_recv)
+    def come_out(group, d):
+        m = turn(x, NX - d, NX)
+        copy(piece(c, m, group), piece(c, m, group), out_s.at[d - 1, group], out_r.at[d - 1, group], at(x=m)).wait_recv()
+
+    def come_shared(group, d):
+        m = turn(x, NX - d, NX)
+        copy(piece(1 - c, m, group), piece(1 - c, m, group), sib_s.at[d, group], sib_r.at[d, group], sibling).wait_recv()
+
+    for d in (1, 3, 2):
+        come_out(0, d)
+        share(0, d)
+
+    opposite.wait_recv()
+    near = copy(ep, sink.at[c], sink_s, sink_r.at[c], sibling)
+    far = copy(es.at[:, zh], sink.at[c], sink_s, sink_r.at[c], sibling)
+
+    @pl.when(c == zh)
+    def _():
+        near.start()
+        for m in range(NY):
+            sink[c, m] = es[m, zh]
+
+    @pl.when(c != zh)
+    def _():
+        far.start()
+        sink[c] = ep[...]
+
+    sends.append(near)
+
+    for group in (1, 2):
+        for d in (1, 3, 2):
+            come_out(group, d)
+            share(group, d)
+
+    copy(ep, sink.at[1 - c], sink_s, sink_r.at[1 - c], sibling).wait_recv()
     for t in range(2):
         left = sink[t].astype(F32).reshape(NY * ROWS, COLS).astype(BF16)
         for s in range(2):
@@ -299,63 +327,50 @@
                 for m in range(NY):
                     half[s, m, 4 * t + k] = value[m]
 
-    def come_out(group, d):
-        m = turn(x, NX - d, NX)
-        copy(piece(c, m, group), piece(c, m, group), out_s.at[d - 1, group], out_r.at[d - 1, group], at(x=m)).wait_recv()
-
-    def come_shared(group, d):
-        m = turn(x, NX - d, NX)
-        copy(piece(1 - c, m, group), piece(1 - c, m, group), sib_s.at[d, group], sib_r.at[d, group], sibling).wait_recv()
-
 
     def flat(value):
         return value.astype(F32).reshape(NEV, COLS).astype(BF16)
 
     def finish(s, d):
-        slot, m = d, turn(x, NX - d, NX)
-        rows = flat(src[s, m])
-        both[slot % 2, :NEV] = rows
-        both[slot % 2, NEV:] = jnp.dot(rows, swap, preferred_element_type=F32).astype(BF16)
-        value = lax.dot_general(
-            flat(half[s, m]), both[slot % 2], (((1,), (1,)), ((), ())), preferred_element_type=F32
-        )
+        slot, m = d % 2, turn(x, NX - d, NX)
+        heights = [(b % 2) * ZLO + b // 2 for b in range(NZ)]
+        rows = [src[s, m, turn(height + NZ, -z, NZ)].astype(F32) for height in heights]
+        rows = jnp.concatenate(rows, axis=0).astype(BF16)
+        both[slot, :NEV] = rows
+        both[slot, NEV:] = jnp.dot(rows, swap, preferred_element_type=F32).astype(BF16)
+        value = lax.dot_general(flat(half[s, m]), both[slot], (((1,), (1,)), ((), ())), preferred_element_type=F32)
         value = value.reshape(2, 4, ROWS, COLS)
         for t in range(2):
             blocks[m, t, s] = value[t]
 
-    early = 3
-    for group in range(early):
-        for d in (1, 3, 2):
-            come_out(group, d)
-            share(group, d)
     finish(c, 0)
-    for group in range(NZ):
+    for group in range(4):
         come_shared(group, 0)
     finish(1 - c, 0)
-    for group in range(early, NZ):
-        for d in (1, 3, 2):
-            come_out(group, d)
-            share(group, d)
+    for d in (1, 3, 2):
+        come_out(3, d)
+        share(3, d)
     for d in (1, 3, 2):
         finish(c, d)
     for d in (1, 3, 2):
-        for group in range(NZ):
+        for group in range(4):
             come_shared(group, d)
         finish(1 - c, d)
 
     for each in sends:
         each.wait_send()
-    pl.when(c != zh)(to_sibling.wait_send)
 
     @pl.when(x != y)
     def _():
         to_pick.wait_send()
-        to_diagonal.wait_send()
+        to_diagonal(0).wait_send()
+
+    to_diagonal(1).wait_send()
 
     @pl.when(picks)
     def _():
-        for dy, ds in moves:
-            pick(dy, ds).wait_send()
+        for dy in (2, 1, 3):
+            pick(dy).wait_send()
 
 
 def exchanged(eigvecs, momenta, source_times, perambulator):
@@ -374,12 +389,13 @@
             pltpu.VMEM((2, SITES, COLS), BF16), pltpu.SMEM((NY, 3), jnp.int32), pltpu.SMEM((2,), jnp.int32),
             pltpu.VMEM((SITES, 8), F32), pltpu.VMEM((2, COLS, SITES), BF16), pltpu.VMEM((2, SITES, COLS), BF16),
             pltpu.VMEM((2, SITES, COLS), BF16),
-            vmem(4, 8), vmem(4, 8), vmem(4, 8, kind=F32), vmem(3, 8), vmem(3, 8), vmem(8), vmem(8), vmem(2), vmem(4, 2),
-            pltpu.VMEM((4, 2, 8, COLS), jnp.int32), vmem(4, 2), vmem(2), vmem(2, 4),
+            vmem(4, 8), vmem(4, 8), vmem(4, 8, kind=F32), vmem(3, 8), vmem(3, 8), vmem(8), vmem(8), vmem(4, 2, 2),
+            pltpu.VMEM((4, 2, 8, COLS), jnp.int32), vmem(4), vmem(4, 2), vmem(4), vmem(2, 4),
             pltpu.VMEM((2, 2, 4, COLS, COLS), BF16),
             dma((4,)), dma((2, 2)), dma((4,)), dma((4,)), dma, dma((4,)), dma((3,)), dma((3,)), dma((8,)), dma((8,)),
-            dma, dma((4,)), dma((4, 2)), dma((2, 4)), dma((4, 2)), dma((2,)),
-            dma((8,)), dma((8,)), dma((3, 8)), dma((3, 8)), dma((4, 8)), dma((4, 8)),
+            dma((2,)), dma((4, 2)), dma((4,)), dma,
+            dma((3,)), dma((4,)), dma, dma, dma, dma((2,)), dma((8,)), dma((8,)),
+            dma((3, 4)), dma((3, 4)), dma((4, 4)), dma((4, 4)),
         ],
         compiler_params=pltpu.CompilerParams(
             collective_id=0, has_side_effects=True, vmem_limit_bytes=50 * 1024 * 1024

time: 53.9 us -> 51.8 us (0.961)
  Pallas kernels: 52.4 us -> 50.3 us
    pallas_call x1, Pallas kernels: 52.4 us -> 50.3 us  [exchanged(): pl.pallas_call(exchange, out_shape=jax.ShapeDtypeStruct((NY, 2, 2, 4, ROW...]
where the time goes in v5:
time: 51.8 us; the launch traced here: 51.7 us
  Pallas kernels  50.3 us (97%)
  local copies, waits for them, and re-layouts  1.41 us (3%)
    pallas_call x1, Pallas kernels, exchanged(): pl.pallas_call(exchange, out_shape=jax.ShapeDtypeStruct((NY, 2, 2, 4, ROW...  50.3 us
    unnamed x1, local copies, waits for them, and re-layouts  1.41 us

profile of v5, /device:TPU:1, one launch (start us, length us, event | category | flops | bytes accessed | tf_op | source)
XLA Modules:
  0.0 51.7 jit_solution(7011285346353895557)
XLA Ops:
  0.0 50.3 %shard_map.46 = f32[4,2,2,4,24,384]{5,4,3,2,1,0:T(8,128)S(1)} custom-call(bf16[2,1024,384]{2,1,0:T(8,128)(2,1)} %eigvecs.1, s32[4,3]{1,0:T(4,128)} %momenta.1, s32[2]{0:T(128)} %source_times.1, bf16[2,2,4,192,384]{4,3,2,1,0:T(8,128)(2,1)} %peram.1), custom_call_target="tpu_custom_call" | custom-call | tf_op jit(solution)/shard_map/pallas_call | solution.py:382
  50.3 1.4 %copy.6 = f32[4,2,2,4,24,384]{5,4,3,2,1,0:T(8,128)} copy(f32[4,2,2,4,24,384]{5,4,3,2,1,0:T(8,128)S(1)} %shard_map.46) | data formatting | bytes 4718592

commit v6 on v5

--- a/solution.py
+++ b/solution.py
@@ -48,7 +48,6 @@
     zh, x = lax.div(snk, NX), lax.rem(snk, NX)
     zl, c = lax.div(slab, 2), lax.rem(slab, 2)
     z = zh * ZLO + zl
-    own = block_of(z)
     picks = x == y
 
     def at(y=y, x=x, z=None, zh=zh, zl=zl, c=c):
@@ -128,12 +127,20 @@
     def time(other):
         return 1 - c if other else c
 
-    def go_along(d):
+    slots = [turn((b % 2) * ZLO + b // 2 + 2 * NZ - 2, -z, NZ) for b in range(NZ)]
+
+    def ready(d):
         pair[d].wait_recv()
-        ysend[d - 1] = (mine[d] + d2d[d].astype(F32)).astype(BF16)
-        along[d] = copy(ysend.at[d - 1], yrecv.at[d - 1], y_s.at[d - 1], y_r.at[d - 1], at(y=turn(y, d, NY)))
-        along[d].start()
-
+        for b in range(NZ):
+            ysend[d - 1, slots[b]] = (mine[d, b] + d2d[d, b].astype(F32)).astype(BF16)
+
+    def go_along(d, part):
+        there = pl.ds(4 * part, 4)
+        along[d, part] = copy(ysend.at[d - 1, there], yrecv.at[d - 1, there], y_s.at[d - 1, part],
+                              y_r.at[d - 1, part], at(y=turn(y, d, NY)))
+        along[d, part].start()
+
+    after = {2: ((2, 0),), 1: ((1, 0), (2, 1)), 3: ((3, 0), (1, 1), (3, 1))}
     phase(1 - c, 2, 0)
     for k, (other, d) in enumerate(turns):
         if k == 1:
@@ -162,9 +169,10 @@
         elif k and other:
             pair[d].start()
         elif k and d:
-            go_along(d)
-    along = [along[d] for d in (2, 1, 3)]
-    sends += list(pair.values()) + along
+            ready(d)
+            for each in after[d]:
+                go_along(*each)
+    sends += list(pair.values()) + list(along.values())
 
     for each in loads:
         each.wait()
@@ -174,22 +182,23 @@
                 pcat[t, s, k, NEV:] = jnp.dot(pcat[t, s, k, :NEV], swap, preferred_element_type=F32).astype(BF16)
 
     pair[0].wait_recv()
-    for each in along:
-        each.wait_recv()
-
-    def summed(block):
+
+    def summed(r):
+        block = block_of(turn(z, r, NZ))
         total = mine[0, block] + d2d[0, block].astype(F32)
         for d in range(3):
-            total += yrecv[d, block].astype(F32)
+            total += yrecv[d, (r + 6) % NZ].astype(F32)
         return total.astype(BF16)
 
-    for dz in (4, 3, 5, 2, 6, 1, 7):
-        to = turn(z, dz, NZ)
-        q[dz] = summed(block_of(to))
-        each = copy(q.at[dz], zrecv.at[z], z_s.at[dz], z_r.at[z], at(z=to))
-        each.start()
-        sends.append(each)
-    zrecv[z] = summed(own)
+    for part, heights in ((0, (4, 3, 5, 2)), (1, (6, 1, 7))):
+        for d in (2, 1, 3):
+            along[d, part].wait_recv()
+        for dz in heights:
+            q[dz] = summed(dz)
+            each = copy(q.at[dz], zrecv.at[z], z_s.at[dz], z_r.at[z], at(z=turn(z, dz, NZ)))
+            each.start()
+            sends.append(each)
+    zrecv[z] = summed(0)
     for dz in range(1, NZ):
         come = turn(z, dz, NZ)
         copy(q.at[dz], zrecv.at[come], z_s.at[dz], z_r.at[come], at(z=come)).wait_recv()
@@ -241,6 +250,13 @@
             pick(dy).start()
         src[c, x, 0] = picked(y)
 
+    for d in (1, 2, 3):
+        m = turn(y, d, NY)
+        copy(es.at[m], es.at[m], es_s.at[d - 1], es_r.at[m], at(y=m)).wait_recv()
+    opposite = copy(es.at[:, 1 - zh], ep, ep_s, ep_r, at(z=turn(z, ZLO, NZ)))
+    opposite.start()
+    sends.append(opposite)
+
     @pl.when(x != y)
     def _():
         pick(1).wait_recv()
@@ -271,14 +287,7 @@
 
     spread(0)
 
-    for d in (1, 2, 3):
-        m = turn(y, d, NY)
-        copy(es.at[m], es.at[m], es_s.at[d - 1], es_r.at[m], at(y=m)).wait_recv()
-    opposite = copy(es.at[:, 1 - zh], ep, ep_s, ep_r, at(z=turn(z, ZLO, NZ)))
-    opposite.start()
-    sends.append(opposite)
-
-    for group in (1, 2, 3):
+    def come_up(group):
         for k in range(groups[group][0], sum(groups[group])):
             copy(src.at[c, x, 0], src.at[c, x, k], up_s.at[1], up_r.at[k], at(z=turn(z, k, NZ))).wait_recv()
         spread(group)
@@ -291,10 +300,6 @@
         m = turn(x, NX - d, NX)
         copy(piece(1 - c, m, group), piece(1 - c, m, group), sib_s.at[d, group], sib_r.at[d, group], sibling).wait_recv()
 
-    for d in (1, 3, 2):
-        come_out(0, d)
-        share(0, d)
-
     opposite.wait_recv()
     near = copy(ep, sink.at[c], sink_s, sink_r.at[c], sibling)
     far = copy(es.at[:, zh], sink.at[c], sink_s, sink_r.at[c], sibling)
@@ -311,11 +316,8 @@
         sink[c] = ep[...]
 
     sends.append(near)
-
-    for group in (1, 2):
-        for d in (1, 3, 2):
-            come_out(group, d)
-            share(group, d)
+    come_up(1)
+    come_up(2)
 
     copy(ep, sink.at[1 - c], sink_s, sink_r.at[1 - c], sibling).wait_recv()
     for t in range(2):
@@ -326,6 +328,12 @@
                 value = value.reshape(NY, ROWS, COLS).astype(BF16)
                 for m in range(NY):
                     half[s, m, 4 * t + k] = value[m]
+
+    come_up(3)
+    for group in (0, 1, 2):
+        for d in (1, 3, 2):
+            come_out(group, d)
+            share(group, d)
 
 
     def flat(value):
@@ -392,7 +400,7 @@
             vmem(4, 8), vmem(4, 8), vmem(4, 8, kind=F32), vmem(3, 8), vmem(3, 8), vmem(8), vmem(8), vmem(4, 2, 2),
             pltpu.VMEM((4, 2, 8, COLS), jnp.int32), vmem(4), vmem(4, 2), vmem(4), vmem(2, 4),
             pltpu.VMEM((2, 2, 4, COLS, COLS), BF16),
-            dma((4,)), dma((2, 2)), dma((4,)), dma((4,)), dma, dma((4,)), dma((3,)), dma((3,)), dma((8,)), dma((8,)),
+            dma((4,)), dma((2, 2)), dma((4,)), dma((4,)), dma, dma((4,)), dma((3, 2)), dma((3, 2)), dma((8,)), dma((8,)),
             dma((2,)), dma((4, 2)), dma((4,)), dma,
             dma((3,)), dma((4,)), dma, dma, dma, dma((2,)), dma((8,)), dma((8,)),
             dma((3, 4)), dma((3, 4)), dma((4, 4)), dma((4, 4)),

time: 51.8 us -> 50.7 us (0.979)
  Pallas kernels: 50.3 us -> 49.2 us
    pallas_call x1, Pallas kernels: 50.3 us -> 49.2 us  [exchanged(): pl.pallas_call(exchange, out_shape=jax.ShapeDtypeStruct((NY, 2, 2, 4, ROW...]
where the time goes in v6:
time: 50.7 us; the launch traced here: 50.6 us
  Pallas kernels  49.2 us (97%)
  local copies, waits for them, and re-layouts  1.41 us (3%)
    pallas_call x1, Pallas kernels, exchanged(): pl.pallas_call(exchange, out_shape=jax.ShapeDtypeStruct((NY, 2, 2, 4, ROW...  49.2 us
    unnamed x1, local copies, waits for them, and re-layouts  1.41 us

profile of v6, /device:TPU:1, one launch (start us, length us, event | category | flops | bytes accessed | tf_op | source)
XLA Modules:
  0.0 50.6 jit_solution(16480999958426236249)
XLA Ops:
  0.0 49.2 %shard_map.46 = f32[4,2,2,4,24,384]{5,4,3,2,1,0:T(8,128)S(1)} custom-call(bf16[2,1024,384]{2,1,0:T(8,128)(2,1)} %eigvecs.1, s32[4,3]{1,0:T(4,128)} %momenta.1, s32[2]{0:T(128)} %source_times.1, bf16[2,2,4,192,384]{4,3,2,1,0:T(8,128)(2,1)} %peram.1), custom_call_target="tpu_custom_call" | custom-call | tf_op jit(solution)/shard_map/pallas_call | solution.py:390
  49.2 1.4 %copy.6 = f32[4,2,2,4,24,384]{5,4,3,2,1,0:T(8,128)} copy(f32[4,2,2,4,24,384]{5,4,3,2,1,0:T(8,128)S(1)} %shard_map.46) | data formatting | bytes 4718592

commit v7 on v6

--- a/solution.py
+++ b/solution.py
@@ -41,7 +41,7 @@
 def exchange(eigvecs, momenta, source_times, peram, blocks, src, half, both, eig, mom, st, trig, vt, vs, w, dsend, d2d,
              mine, ysend, yrecv, q, zrecv, xall, stall, sel, es, ep, sink, pcat,
              in_s, p_s, d2d_s, d2d_r, st_s, st_r, y_s, y_r, z_s, z_r, x_s, x_r, sel_s, sel_r,
-             es_s, es_r, ep_s, ep_r, sink_s, sink_r, up_s, up_r, out_s, out_r, sib_s, sib_r):
+             es_s, es_r, ep_s, ep_r, sink_s, sink_r, up_s, up_r, out_s, out_r, sib_s, sib_r, known):
     y = lax.axis_index("src")
     snk = lax.axis_index("snk")
     slab = lax.axis_index("slab")
@@ -77,12 +77,15 @@
         each.start()
 
     barrier = pltpu.get_barrier_semaphore()
-    peers = [at(z=turn(z, k, NZ)) for k in (4, 3, 5)] + [at(x=turn(x, 2, NX), c=k) for k in range(2)]
-    peers += [at(y=turn(y, 2, NY))] + [at(z=turn(z, k, NZ)) for k in (2, 6)]
-    peers += [at(x=turn(x, d, NX), c=k) for d in (1, 3) for k in range(2)]
-    peers += [at(y=turn(y, d, NY)) for d in (1, 3)] + [at(z=turn(z, k, NZ)) for k in (1, 7)] + [at(c=1 - c)]
+    peers = [at(y=turn(y, d, NY)) for d in (2, 1, 3)] + [at(z=turn(z, k, NZ)) for k in (1, 7)]
+    peers += [at(x=turn(x, d, NX)) for d in (1, 3)] + [at(c=1 - c)]
     for peer in peers:
         pl.semaphore_signal(barrier, inc=1, device_id=peer, device_id_type=MESH)
+
+    def tell(round, height):
+        for peer in [at(z=turn(z, k, NZ)) for k in (height, NZ - height)] + [at(x=turn(x, d, NX)) for d in (1, 3)]:
+            pl.semaphore_signal(known.at[round], inc=1, device_id=peer, device_id_type=MESH)
+
     fetches[0].wait()
     fetches[2].wait()
 
@@ -140,7 +143,6 @@
                               y_r.at[d - 1, part], at(y=turn(y, d, NY)))
         along[d, part].start()
 
-    after = {2: ((2, 0),), 1: ((1, 0), (2, 1)), 3: ((3, 0), (1, 1), (3, 1))}
     phase(1 - c, 2, 0)
     for k, (other, d) in enumerate(turns):
         if k == 1:
@@ -157,21 +159,30 @@
             pair[d] = copy(dsend.at[d], d2d.at[d], d2d_s.at[d], d2d_r.at[d], sibling)
         else:
             mine[d] = value
-        if k == 1:
+        if k == 3:
             pl.semaphore_wait(barrier, len(peers))
-            for each in (2, 1):
+            for each in (2, 1, 3):
                 pair[each].start()
+            tell(0, 1)
             fetches[1].wait()
             for s in range(2):
                 stall[y, s] = jnp.full((8, COLS), st[s], jnp.int32)
             to_pick = copy(stall.at[y], stall.at[y], st_s, st_r.at[y], at(y=x))
             pl.when(x != y)(to_pick.start)
-        elif k and other:
-            pair[d].start()
-        elif k and d:
-            ready(d)
-            for each in after[d]:
+        if k == 4:
+            ready(2)
+            go_along(2, 0)
+            ready(1)
+            go_along(1, 0)
+            go_along(2, 1)
+        if k == 5:
+            ready(3)
+            for each in ((3, 0), (1, 1), (3, 1)):
                 go_along(*each)
+            pl.semaphore_wait(known.at[0], 4)
+            tell(1, 2)
+        if k == 6:
+            pair[0].start()
     sends += list(pair.values()) + list(along.values())
 
     for each in loads:
@@ -182,6 +193,7 @@
                 pcat[t, s, k, NEV:] = jnp.dot(pcat[t, s, k, :NEV], swap, preferred_element_type=F32).astype(BF16)
 
     pair[0].wait_recv()
+    pl.semaphore_wait(known.at[1], 4)
 
     def summed(r):
         block = block_of(turn(z, r, NZ))
@@ -403,7 +415,7 @@
             dma((4,)), dma((2, 2)), dma((4,)), dma((4,)), dma, dma((4,)), dma((3, 2)), dma((3, 2)), dma((8,)), dma((8,)),
             dma((2,)), dma((4, 2)), dma((4,)), dma,
             dma((3,)), dma((4,)), dma, dma, dma, dma((2,)), dma((8,)), dma((8,)),
-            dma((3, 4)), dma((3, 4)), dma((4, 4)), dma((4, 4)),
+            dma((3, 4)), dma((3, 4)), dma((4, 4)), dma((4, 4)), pltpu.SemaphoreType.REGULAR((2,)),
         ],
         compiler_params=pltpu.CompilerParams(
             collective_id=0, has_side_effects=True, vmem_limit_bytes=50 * 1024 * 1024

time: 50.7 us -> 50.9 us (level)
  no operation moved by 1% of the time
where the time goes in v7:
time: 50.9 us; the launch traced here: 50.8 us
  Pallas kernels  49.4 us (97%)
  local copies, waits for them, and re-layouts  1.41 us (3%)
    pallas_call x1, Pallas kernels, exchanged(): pl.pallas_call(exchange, out_shape=jax.ShapeDtypeStruct((NY, 2, 2, 4, ROW...  49.4 us
    unnamed x1, local copies, waits for them, and re-layouts  1.41 us

profile of v7, /device:TPU:1, one launch (start us, length us, event | category | flops | bytes accessed | tf_op | source)
XLA Modules:
  0.0 50.8 jit_solution(9744150175450113469)
XLA Ops:
  0.0 49.4 %shard_map.46 = f32[4,2,2,4,24,384]{5,4,3,2,1,0:T(8,128)S(1)} custom-call(bf16[2,1024,384]{2,1,0:T(8,128)(2,1)} %eigvecs.1, s32[4,3]{1,0:T(4,128)} %momenta.1, s32[2]{0:T(128)} %source_times.1, bf16[2,2,4,192,384]{4,3,2,1,0:T(8,128)(2,1)} %peram.1), custom_call_target="tpu_custom_call" | custom-call | tf_op jit(solution)/shard_map/pallas_call | solution.py:402
  49.4 1.4 %copy.6 = f32[4,2,2,4,24,384]{5,4,3,2,1,0:T(8,128)} copy(f32[4,2,2,4,24,384]{5,4,3,2,1,0:T(8,128)S(1)} %shard_map.46) | data formatting | bytes 4718592

commit v8 on v6

--- a/solution.py
+++ b/solution.py
@@ -39,16 +39,15 @@
 
 
 def exchange(eigvecs, momenta, source_times, peram, blocks, src, half, both, eig, mom, st, trig, vt, vs, w, dsend, d2d,
-             mine, ysend, yrecv, q, zrecv, xall, stall, sel, es, ep, sink, pcat,
-             in_s, p_s, d2d_s, d2d_r, st_s, st_r, y_s, y_r, z_s, z_r, x_s, x_r, sel_s, sel_r,
-             es_s, es_r, ep_s, ep_r, sink_s, sink_r, up_s, up_r, out_s, out_r, sib_s, sib_r):
+             mine, ysend, yrecv, q, zrecv, wanted, sel, srecv, es, ep, sink, pcat,
+             in_s, p_s, d2d_s, d2d_r, y_s, y_r, z_s, z_r, sel_s, sel_r,
+             es_s, es_r, ep_s, ep_r, sink_s, sink_r, up_s, up_r, out_s, out_r, sib_s, sib_r, known):
     y = lax.axis_index("src")
     snk = lax.axis_index("snk")
     slab = lax.axis_index("slab")
     zh, x = lax.div(snk, NX), lax.rem(snk, NX)
     zl, c = lax.div(slab, 2), lax.rem(slab, 2)
     z = zh * ZLO + zl
-    picks = x == y
 
     def at(y=y, x=x, z=None, zh=zh, zl=zl, c=c):
         if z is not None:
@@ -77,12 +76,15 @@
         each.start()
 
     barrier = pltpu.get_barrier_semaphore()
-    peers = [at(z=turn(z, k, NZ)) for k in (4, 3, 5)] + [at(x=turn(x, 2, NX), c=k) for k in range(2)]
-    peers += [at(y=turn(y, 2, NY))] + [at(z=turn(z, k, NZ)) for k in (2, 6)]
-    peers += [at(x=turn(x, d, NX), c=k) for d in (1, 3) for k in range(2)]
-    peers += [at(y=turn(y, d, NY)) for d in (1, 3)] + [at(z=turn(z, k, NZ)) for k in (1, 7)] + [at(c=1 - c)]
+    peers = [at(y=turn(y, d, NY)) for d in (2, 1, 3)] + [at(z=turn(z, k, NZ)) for k in (1, 7)]
+    peers += [at(x=turn(x, d, NX)) for d in (1, 3)] + [at(c=1 - c)]
     for peer in peers:
         pl.semaphore_signal(barrier, inc=1, device_id=peer, device_id_type=MESH)
+
+    def tell(round, height):
+        for peer in [at(z=turn(z, k, NZ)) for k in (height, NZ - height)] + [at(x=turn(x, d, NX)) for d in (1, 3)]:
+            pl.semaphore_signal(known.at[round], inc=1, device_id=peer, device_id_type=MESH)
+
     fetches[0].wait()
     fetches[2].wait()
 
@@ -161,17 +163,16 @@
             pl.semaphore_wait(barrier, len(peers))
             for each in (2, 1):
                 pair[each].start()
-            fetches[1].wait()
-            for s in range(2):
-                stall[y, s] = jnp.full((8, COLS), st[s], jnp.int32)
-            to_pick = copy(stall.at[y], stall.at[y], st_s, st_r.at[y], at(y=x))
-            pl.when(x != y)(to_pick.start)
+            tell(0, 1)
         elif k and other:
             pair[d].start()
         elif k and d:
             ready(d)
             for each in after[d]:
                 go_along(*each)
+        if k == 6:
+            pl.semaphore_wait(known.at[0], 4)
+            tell(1, 2)
     sends += list(pair.values()) + list(along.values())
 
     for each in loads:
@@ -182,6 +183,7 @@
                 pcat[t, s, k, NEV:] = jnp.dot(pcat[t, s, k, :NEV], swap, preferred_element_type=F32).astype(BF16)
 
     pair[0].wait_recv()
+    pl.semaphore_wait(known.at[1], 4)
 
     def summed(r):
         block = block_of(turn(z, r, NZ))
@@ -208,58 +210,43 @@
             total += zrecv[g * ZLO + k].astype(F32)
         es[y, g] = total.astype(BF16)
 
-    def to_diagonal(k):
-        return copy(es.at[y], xall.at[x, c], x_s.at[k], x_r.at[x, c], at(x=y, c=turn(c, k, 2)))
-
-    @pl.when(x != y)
-    def _():
-        for k in range(2):
-            to_diagonal(k).start()
-
     for d in (2, 1, 3):
         each = copy(es.at[y], es.at[y], es_s.at[d - 1], es_r.at[y], at(y=turn(y, d, NY)))
         each.start()
         sends.append(each)
-
-    def picked(plane):
-        wanted = stall[plane, c][0:1]
-        total = jnp.zeros((ROWS, COLS), F32)
-        for k in range(NX):
-            for parity in range(2):
-                for g in range(2):
-                    total += jnp.where(wanted == 2 * (g * NX + k) + parity, xall[k, parity, g].astype(F32), 0.0)
-        return total.astype(BF16)
-
-    def pick(dy):
-        return copy(sel.at[dy], src.at[c, x, 0], sel_s.at[dy], sel_r, at(y=turn(y, dy, NY)))
-
-    @pl.when(picks)
-    def _():
-        to_diagonal(1).start()
-        xall[x, c] = es[y]
-        for d in (0, 1, 3, 2):
-            for k in range(2):
-                if d or k:
-                    come, parity = turn(x, d, NX), turn(c, k, 2)
-                    copy(es.at[y], xall.at[come, parity], x_s.at[k], x_r.at[come, parity], at(x=come, c=1 - c)).wait_recv()
-            if d:
-                come = turn(y, d, NY)
-                copy(stall.at[come], stall.at[come], st_s, st_r.at[come], at(y=come)).wait_recv()
-        for dy in (2, 1, 3):
-            sel[dy] = picked(turn(y, dy, NY))
-            pick(dy).start()
-        src[c, x, 0] = picked(y)
-
-    for d in (1, 2, 3):
+    fetches[1].wait()
+    for s in range(2):
+        wanted[s] = jnp.full((8, COLS), st[s], jnp.int32)
+    for d in (1, 3, 2):
         m = turn(y, d, NY)
         copy(es.at[m], es.at[m], es_s.at[d - 1], es_r.at[m], at(y=m)).wait_recv()
+
+    def picked(m, s):
+        total = jnp.zeros((ROWS, COLS), F32)
+        for g in range(2):
+            total += jnp.where(wanted[s][0:1] == 2 * (g * NX + x) + c, es[m, g].astype(F32), 0.0)
+        return total.astype(BF16)
+
+    for d, k in ((2, 0), (2, 1), (1, 0), (1, 1), (3, 0), (3, 1), (0, 1)):
+        m, s = turn(x, d, NX), turn(c, k, 2)
+        sel[d, k] = picked(m, s)
+        each = copy(sel.at[d, k], srecv.at[x, c], sel_s.at[d, k], sel_r.at[x, c], at(x=m, c=s))
+        each.start()
+        sends.append(each)
+
     opposite = copy(es.at[:, 1 - zh], ep, ep_s, ep_r, at(z=turn(z, ZLO, NZ)))
     opposite.start()
     sends.append(opposite)
 
-    @pl.when(x != y)
-    def _():
-        pick(1).wait_recv()
+    srecv[x, c] = picked(x, c)
+    for d, k in ((0, 1), (1, 0), (1, 1), (3, 0), (3, 1), (2, 0), (2, 1)):
+        come, core = turn(x, d, NX), turn(c, k, 2)
+        copy(sel.at[d, k], srecv.at[come, core], sel_s.at[d, k], sel_r.at[come, core], at(x=come, c=core) if d else sibling).wait_recv()
+    total = jnp.zeros((ROWS, COLS), F32)
+    for k in range(NX):
+        for core in range(2):
+            total += srecv[k, core].astype(F32)
+    src[c, x, 0] = total.astype(BF16)
 
     groups = ((0, 1), (1, 2), (6, 2), (3, 3))
 
@@ -368,18 +355,6 @@
     for each in sends:
         each.wait_send()
 
-    @pl.when(x != y)
-    def _():
-        to_pick.wait_send()
-        to_diagonal(0).wait_send()
-
-    to_diagonal(1).wait_send()
-
-    @pl.when(picks)
-    def _():
-        for dy in (2, 1, 3):
-            pick(dy).wait_send()
-
 
 def exchanged(eigvecs, momenta, source_times, perambulator):
     dma = pltpu.SemaphoreType.DMA
@@ -397,13 +372,13 @@
             pltpu.VMEM((2, SITES, COLS), BF16), pltpu.SMEM((NY, 3), jnp.int32), pltpu.SMEM((2,), jnp.int32),
             pltpu.VMEM((SITES, 8), F32), pltpu.VMEM((2, COLS, SITES), BF16), pltpu.VMEM((2, SITES, COLS), BF16),
             pltpu.VMEM((2, SITES, COLS), BF16),
-            vmem(4, 8), vmem(4, 8), vmem(4, 8, kind=F32), vmem(3, 8), vmem(3, 8), vmem(8), vmem(8), vmem(4, 2, 2),
-            pltpu.VMEM((4, 2, 8, COLS), jnp.int32), vmem(4), vmem(4, 2), vmem(4), vmem(2, 4),
+            vmem(4, 8), vmem(4, 8), vmem(4, 8, kind=F32), vmem(3, 8), vmem(3, 8), vmem(8), vmem(8),
+            pltpu.VMEM((2, 8, COLS), jnp.int32), vmem(4, 2), vmem(4, 2), vmem(4, 2), vmem(4), vmem(2, 4),
             pltpu.VMEM((2, 2, 4, COLS, COLS), BF16),
-            dma((4,)), dma((2, 2)), dma((4,)), dma((4,)), dma, dma((4,)), dma((3, 2)), dma((3, 2)), dma((8,)), dma((8,)),
-            dma((2,)), dma((4, 2)), dma((4,)), dma,
+            dma((4,)), dma((2, 2)), dma((4,)), dma((4,)), dma((3, 2)), dma((3, 2)), dma((8,)), dma((8,)),
+            dma((4, 2)), dma((4, 2)),
             dma((3,)), dma((4,)), dma, dma, dma, dma((2,)), dma((8,)), dma((8,)),
-            dma((3, 4)), dma((3, 4)), dma((4, 4)), dma((4, 4)),
+            dma((3, 4)), dma((3, 4)), dma((4, 4)), dma((4, 4)), pltpu.SemaphoreType.REGULAR((2,)),
         ],
         compiler_params=pltpu.CompilerParams(
             collective_id=0, has_side_effects=True, vmem_limit_bytes=50 * 1024 * 1024

time: 50.7 us -> 49.9 us (0.984)
  Pallas kernels: 49.2 us -> 48.4 us
    pallas_call x1, Pallas kernels: 49.2 us -> 48.4 us  [exchanged(): pl.pallas_call(exchange, out_shape=jax.ShapeDtypeStruct((NY, 2, 2, 4, ROW...]
where the time goes in v8:
time: 49.9 us; the launch traced here: 49.8 us
  Pallas kernels  48.4 us (97%)
  local copies, waits for them, and re-layouts  1.41 us (3%)
    pallas_call x1, Pallas kernels, exchanged(): pl.pallas_call(exchange, out_shape=jax.ShapeDtypeStruct((NY, 2, 2, 4, ROW...  48.4 us
    unnamed x1, local copies, waits for them, and re-layouts  1.41 us

profile of v8, /device:TPU:1, one launch (start us, length us, event | category | flops | bytes accessed | tf_op | source)
XLA Modules:
  0.0 49.8 jit_solution(6739992818866824970)
XLA Ops:
  0.0 48.4 %shard_map.46 = f32[4,2,2,4,24,384]{5,4,3,2,1,0:T(8,128)S(1)} custom-call(bf16[2,1024,384]{2,1,0:T(8,128)(2,1)} %eigvecs.1, s32[4,3]{1,0:T(4,128)} %momenta.1, s32[2]{0:T(128)} %source_times.1, bf16[2,2,4,192,384]{4,3,2,1,0:T(8,128)(2,1)} %peram.1), custom_call_target="tpu_custom_call" | custom-call | tf_op jit(solution)/shard_map/pallas_call | solution.py:365
  48.4 1.4 %copy.6 = f32[4,2,2,4,24,384]{5,4,3,2,1,0:T(8,128)} copy(f32[4,2,2,4,24,384]{5,4,3,2,1,0:T(8,128)S(1)} %shard_map.46) | data formatting | bytes 4718592

commit v9 on v8

--- a/solution.py
+++ b/solution.py
@@ -39,9 +39,9 @@
 
 
 def exchange(eigvecs, momenta, source_times, peram, blocks, src, half, both, eig, mom, st, trig, vt, vs, w, dsend, d2d,
-             mine, ysend, yrecv, q, zrecv, wanted, sel, srecv, es, ep, sink, pcat,
+             mine, ysend, yrecv, q, zrecv, wanted, sel, srecv, es, ep, sink, pcat, zearly, far, come,
              in_s, p_s, d2d_s, d2d_r, y_s, y_r, z_s, z_r, sel_s, sel_r,
-             es_s, es_r, ep_s, ep_r, sink_s, sink_r, up_s, up_r, out_s, out_r, sib_s, sib_r, known):
+             es_s, es_r, ep_s, ep_r, sink_s, sink_r, up_s, up_r, out_s, out_r, sib_s, sib_r, ze_s, ze_r, far_s, far_r):
     y = lax.axis_index("src")
     snk = lax.axis_index("snk")
     slab = lax.axis_index("slab")
@@ -76,15 +76,12 @@
         each.start()
 
     barrier = pltpu.get_barrier_semaphore()
-    peers = [at(y=turn(y, d, NY)) for d in (2, 1, 3)] + [at(z=turn(z, k, NZ)) for k in (1, 7)]
-    peers += [at(x=turn(x, d, NX)) for d in (1, 3)] + [at(c=1 - c)]
+    peers = [at(z=turn(z, k, NZ)) for k in (4, 3, 5)] + [at(x=turn(x, 2, NX), c=k) for k in range(2)]
+    peers += [at(y=turn(y, 2, NY))] + [at(z=turn(z, k, NZ)) for k in (2, 6)]
+    peers += [at(x=turn(x, d, NX), c=k) for d in (1, 3) for k in range(2)]
+    peers += [at(y=turn(y, d, NY)) for d in (1, 3)] + [at(z=turn(z, k, NZ)) for k in (1, 7)] + [at(c=1 - c)]
     for peer in peers:
         pl.semaphore_signal(barrier, inc=1, device_id=peer, device_id_type=MESH)
-
-    def tell(round, height):
-        for peer in [at(z=turn(z, k, NZ)) for k in (height, NZ - height)] + [at(x=turn(x, d, NX)) for d in (1, 3)]:
-            pl.semaphore_signal(known.at[round], inc=1, device_id=peer, device_id_type=MESH)
-
     fetches[0].wait()
     fetches[2].wait()
 
@@ -142,7 +139,9 @@
                               y_r.at[d - 1, part], at(y=turn(y, d, NY)))
         along[d, part].start()
 
-    after = {2: ((2, 0),), 1: ((1, 0), (2, 1)), 3: ((3, 0), (1, 1), (3, 1))}
+    def early(dz):
+        return copy(ysend.at[1, (dz + 6) % NZ], zearly.at[z], ze_s.at[dz], ze_r.at[z], at(z=turn(z, dz, NZ)))
+
     phase(1 - c, 2, 0)
     for k, (other, d) in enumerate(turns):
         if k == 1:
@@ -163,16 +162,17 @@
             pl.semaphore_wait(barrier, len(peers))
             for each in (2, 1):
                 pair[each].start()
-            tell(0, 1)
         elif k and other:
             pair[d].start()
         elif k and d:
             ready(d)
-            for each in after[d]:
-                go_along(*each)
-        if k == 6:
-            pl.semaphore_wait(known.at[0], 4)
-            tell(1, 2)
+            if d == 2:
+                for dz in (4, 3, 5, 2, 6, 1, 7):
+                    early(dz).start()
+                zearly[z] = ysend[1, 6]
+            else:
+                go_along(d, 0)
+                go_along(d, 1)
     sends += list(pair.values()) + list(along.values())
 
     for each in loads:
@@ -183,29 +183,42 @@
                 pcat[t, s, k, NEV:] = jnp.dot(pcat[t, s, k, :NEV], swap, preferred_element_type=F32).astype(BF16)
 
     pair[0].wait_recv()
-    pl.semaphore_wait(known.at[1], 4)
 
     def summed(r):
         block = block_of(turn(z, r, NZ))
         total = mine[0, block] + d2d[0, block].astype(F32)
-        for d in range(3):
-            total += yrecv[d, (r + 6) % NZ].astype(F32)
+        for d in (1, 3):
+            total += yrecv[d - 1, (r + 6) % NZ].astype(F32)
         return total.astype(BF16)
 
+    to_far = copy(far, come, far_s, far_r, at(y=turn(y, 2, NY)))
+    sends += [early(dz) for dz in range(1, NZ)] + [to_far]
+
     for part, heights in ((0, (4, 3, 5, 2)), (1, (6, 1, 7))):
-        for d in (2, 1, 3):
+        for d in (1, 3):
             along[d, part].wait_recv()
         for dz in heights:
             q[dz] = summed(dz)
             each = copy(q.at[dz], zrecv.at[z], z_s.at[dz], z_r.at[z], at(z=turn(z, dz, NZ)))
             each.start()
             sends.append(each)
+        if part == 0:
+            for dz in range(1, NZ):
+                height = turn(z, dz, NZ)
+                copy(q.at[dz], zearly.at[height], ze_s.at[dz], ze_r.at[height], at(z=height)).wait_recv()
+            for g in range(2):
+                total = zearly[g * ZLO].astype(F32)
+                for k in range(1, ZLO):
+                    total += zearly[g * ZLO + k].astype(F32)
+                far[g] = total.astype(BF16)
+            to_far.start()
     zrecv[z] = summed(0)
     for dz in range(1, NZ):
-        come = turn(z, dz, NZ)
-        copy(q.at[dz], zrecv.at[come], z_s.at[dz], z_r.at[come], at(z=come)).wait_recv()
+        height = turn(z, dz, NZ)
+        copy(q.at[dz], zrecv.at[height], z_s.at[dz], z_r.at[height], at(z=height)).wait_recv()
+    to_far.wait_recv()
     for g in range(2):
-        total = zrecv[g * ZLO].astype(F32)
+        total = zrecv[g * ZLO].astype(F32) + come[g].astype(F32)
         for k in range(1, ZLO):
             total += zrecv[g * ZLO + k].astype(F32)
         es[y, g] = total.astype(BF16)
@@ -240,8 +253,9 @@
 
     srecv[x, c] = picked(x, c)
     for d, k in ((0, 1), (1, 0), (1, 1), (3, 0), (3, 1), (2, 0), (2, 1)):
-        come, core = turn(x, d, NX), turn(c, k, 2)
-        copy(sel.at[d, k], srecv.at[come, core], sel_s.at[d, k], sel_r.at[come, core], at(x=come, c=core) if d else sibling).wait_recv()
+        giver, core = turn(x, d, NX), turn(c, k, 2)
+        copy(sel.at[d, k], srecv.at[giver, core], sel_s.at[d, k], sel_r.at[giver, core],
+             at(x=giver, c=core) if d else sibling).wait_recv()
     total = jnp.zeros((ROWS, COLS), F32)
     for k in range(NX):
         for core in range(2):
@@ -374,11 +388,11 @@
             pltpu.VMEM((2, SITES, COLS), BF16),
             vmem(4, 8), vmem(4, 8), vmem(4, 8, kind=F32), vmem(3, 8), vmem(3, 8), vmem(8), vmem(8),
             pltpu.VMEM((2, 8, COLS), jnp.int32), vmem(4, 2), vmem(4, 2), vmem(4, 2), vmem(4), vmem(2, 4),
-            pltpu.VMEM((2, 2, 4, COLS, COLS), BF16),
+            pltpu.VMEM((2, 2, 4, COLS, COLS), BF16), vmem(8), vmem(2), vmem(2),
             dma((4,)), dma((2, 2)), dma((4,)), dma((4,)), dma((3, 2)), dma((3, 2)), dma((8,)), dma((8,)),
             dma((4, 2)), dma((4, 2)),
             dma((3,)), dma((4,)), dma, dma, dma, dma((2,)), dma((8,)), dma((8,)),
-            dma((3, 4)), dma((3, 4)), dma((4, 4)), dma((4, 4)), pltpu.SemaphoreType.REGULAR((2,)),
+            dma((3, 4)), dma((3, 4)), dma((4, 4)), dma((4, 4)), dma((8,)), dma((8,)), dma, dma,
         ],
         compiler_params=pltpu.CompilerParams(
             collective_id=0, has_side_effects=True, vmem_limit_bytes=50 * 1024 * 1024

time: 49.9 us -> 49.4 us (0.990)
  Pallas kernels: 48.4 us -> 47.9 us
    pallas_call x1, Pallas kernels: 48.4 us -> 47.9 us  [exchanged(): pl.pallas_call(exchange, out_shape=jax.ShapeDtypeStruct((NY, 2, 2, 4, ROW...]
where the time goes in v9:
time: 49.4 us; the launch traced here: 49.3 us
  Pallas kernels  47.9 us (97%)
  local copies, waits for them, and re-layouts  1.41 us (3%)
    pallas_call x1, Pallas kernels, exchanged(): pl.pallas_call(exchange, out_shape=jax.ShapeDtypeStruct((NY, 2, 2, 4, ROW...  47.9 us
    unnamed x1, local copies, waits for them, and re-layouts  1.41 us

profile of v9, /device:TPU:1, one launch (start us, length us, event | category | flops | bytes accessed | tf_op | source)
XLA Modules:
  0.0 49.3 jit_solution(2782022623622598638)
XLA Ops:
  0.0 47.9 %shard_map.46 = f32[4,2,2,4,24,384]{5,4,3,2,1,0:T(8,128)S(1)} custom-call(bf16[2,1024,384]{2,1,0:T(8,128)(2,1)} %eigvecs.1, s32[4,3]{1,0:T(4,128)} %momenta.1, s32[2]{0:T(128)} %source_times.1, bf16[2,2,4,192,384]{4,3,2,1,0:T(8,128)(2,1)} %peram.1), custom_call_target="tpu_custom_call" | custom-call | tf_op jit(solution)/shard_map/pallas_call | solution.py:379
  47.9 1.4 %copy.6 = f32[4,2,2,4,24,384]{5,4,3,2,1,0:T(8,128)} copy(f32[4,2,2,4,24,384]{5,4,3,2,1,0:T(8,128)S(1)} %shard_map.46) | data formatting | bytes 4718592

commit v10 on v9

--- a/solution.py
+++ b/solution.py
@@ -175,13 +175,6 @@
                 go_along(d, 1)
     sends += list(pair.values()) + list(along.values())
 
-    for each in loads:
-        each.wait()
-    for t in range(2):
-        for s in range(2):
-            for k in range(4):
-                pcat[t, s, k, NEV:] = jnp.dot(pcat[t, s, k, :NEV], swap, preferred_element_type=F32).astype(BF16)
-
     pair[0].wait_recv()
 
     def summed(r):
@@ -227,6 +220,13 @@
         each = copy(es.at[y], es.at[y], es_s.at[d - 1], es_r.at[y], at(y=turn(y, d, NY)))
         each.start()
         sends.append(each)
+    for each in loads:
+        each.wait()
+    for t in range(2):
+        for s in range(2):
+            for k in range(4):
+                pcat[t, s, k, NEV:] = jnp.dot(pcat[t, s, k, :NEV], swap, preferred_element_type=F32).astype(BF16)
+
     fetches[1].wait()
     for s in range(2):
         wanted[s] = jnp.full((8, COLS), st[s], jnp.int32)

time: 49.4 us -> 49.2 us (level)
  no operation moved by 1% of the time
where the time goes in v10:
time: 49.2 us; the launch traced here: 49.1 us
  Pallas kernels  47.7 us (97%)
  local copies, waits for them, and re-layouts  1.41 us (3%)
    pallas_call x1, Pallas kernels, exchanged(): pl.pallas_call(exchange, out_shape=jax.ShapeDtypeStruct((NY, 2, 2, 4, ROW...  47.7 us
    unnamed x1, local copies, waits for them, and re-layouts  1.41 us

profile of v10, /device:TPU:1, one launch (start us, length us, event | category | flops | bytes accessed | tf_op | source)
XLA Modules:
  0.0 49.1 jit_solution(6798497444906084663)
XLA Ops:
  0.0 47.7 %shard_map.46 = f32[4,2,2,4,24,384]{5,4,3,2,1,0:T(8,128)S(1)} custom-call(bf16[2,1024,384]{2,1,0:T(8,128)(2,1)} %eigvecs.1, s32[4,3]{1,0:T(4,128)} %momenta.1, s32[2]{0:T(128)} %source_times.1, bf16[2,2,4,192,384]{4,3,2,1,0:T(8,128)(2,1)} %peram.1), custom_call_target="tpu_custom_call" | custom-call | tf_op jit(solution)/shard_map/pallas_call | solution.py:379
  47.7 1.4 %copy.6 = f32[4,2,2,4,24,384]{5,4,3,2,1,0:T(8,128)} copy(f32[4,2,2,4,24,384]{5,4,3,2,1,0:T(8,128)S(1)} %shard_map.46) | data formatting | bytes 4718592

commit v11 on v9

--- a/solution.py
+++ b/solution.py
@@ -262,7 +262,7 @@
             total += srecv[k, core].astype(F32)
     src[c, x, 0] = total.astype(BF16)
 
-    groups = ((0, 1), (1, 2), (6, 2), (3, 3))
+    groups = ((0, 1), (1, 2), (6, 2), (3, 1), (5, 1), (4, 1))
 
     def piece(s, m, group):
         return src.at[s, m, pl.ds(groups[group][0], groups[group][1])]
@@ -330,7 +330,8 @@
                 for m in range(NY):
                     half[s, m, 4 * t + k] = value[m]
 
-    come_up(3)
+    for group in (3, 4, 5):
+        come_up(group)
     for group in (0, 1, 2):
         for d in (1, 3, 2):
             come_out(group, d)
@@ -353,16 +354,17 @@
             blocks[m, t, s] = value[t]
 
     finish(c, 0)
-    for group in range(4):
+    for group in range(6):
         come_shared(group, 0)
     finish(1 - c, 0)
-    for d in (1, 3, 2):
-        come_out(3, d)
-        share(3, d)
+    for group in (3, 4, 5):
+        for d in (1, 3, 2):
+            come_out(group, d)
+            share(group, d)
     for d in (1, 3, 2):
         finish(c, d)
     for d in (1, 3, 2):
-        for group in range(4):
+        for group in range(6):
             come_shared(group, d)
         finish(1 - c, d)
 
@@ -392,7 +394,7 @@
             dma((4,)), dma((2, 2)), dma((4,)), dma((4,)), dma((3, 2)), dma((3, 2)), dma((8,)), dma((8,)),
             dma((4, 2)), dma((4, 2)),
             dma((3,)), dma((4,)), dma, dma, dma, dma((2,)), dma((8,)), dma((8,)),
-            dma((3, 4)), dma((3, 4)), dma((4, 4)), dma((4, 4)), dma((8,)), dma((8,)), dma, dma,
+            dma((3, 6)), dma((3, 6)), dma((4, 6)), dma((4, 6)), dma((8,)), dma((8,)), dma, dma,
         ],
         compiler_params=pltpu.CompilerParams(
             collective_id=0, has_side_effects=True, vmem_limit_bytes=50 * 1024 * 1024

time: 49.4 us -> 49.3 us (level)
  no operation moved by 1% of the time
where the time goes in v11:
time: 49.3 us; the launch traced here: 49.2 us
  Pallas kernels  47.8 us (97%)
  local copies, waits for them, and re-layouts  1.41 us (3%)
    pallas_call x1, Pallas kernels, exchanged(): pl.pallas_call(exchange, out_shape=jax.ShapeDtypeStruct((NY, 2, 2, 4, ROW...  47.8 us
    unnamed x1, local copies, waits for them, and re-layouts  1.41 us

profile of v11, /device:TPU:1, one launch (start us, length us, event | category | flops | bytes accessed | tf_op | source)
XLA Modules:
  0.0 49.2 jit_solution(11729384168326306657)
XLA Ops:
  0.0 47.8 %shard_map.46 = f32[4,2,2,4,24,384]{5,4,3,2,1,0:T(8,128)S(1)} custom-call(bf16[2,1024,384]{2,1,0:T(8,128)(2,1)} %eigvecs.1, s32[4,3]{1,0:T(4,128)} %momenta.1, s32[2]{0:T(128)} %source_times.1, bf16[2,2,4,192,384]{4,3,2,1,0:T(8,128)(2,1)} %peram.1), custom_call_target="tpu_custom_call" | custom-call | tf_op jit(solution)/shard_map/pallas_call | solution.py:381
  47.8 1.4 %copy.6 = f32[4,2,2,4,24,384]{5,4,3,2,1,0:T(8,128)} copy(f32[4,2,2,4,24,384]{5,4,3,2,1,0:T(8,128)S(1)} %shard_map.46) | data formatting | bytes 4718592
